TPU v7x, 512 devices: a whole 4x4x16 slice. The times are simulated.
512 devices in a mesh: row: 16 (over x, y), col: 32 (over z, core).
Axes of the slice: x: 4, y: 4, z: 16, core: 2. Of those that a mesh axis runs over, the one named last changes fastest.
Arguments:
- rhs: float32 [36864, 128], P('row'), may hold values from -6 to 6
- factor: float32 [34816, 4096], P('row', 'col'), may hold values from -0.09375 to 0.09375
- inverses: float32 [2, 2048, 2048], P(None, 'col', 'row'), may hold values from -1 to 3, as said below
Outputs:
- solution: float32 [4096, 128], P('col')
- remaining: float32 [32768, 128], P('row')
Inputs may be any that keep to these rules, and one draw needn't show every extreme that they name: Each inverses[k] is lower triangular in panel order with positive diagonal entries.
All inputs are finite; a program needn't handle non-finite values.
Results may differ from a plain program's by a relative error of at most 0.000068.
Values sent between devices are 32-bit elements; how exact they have to be, the bound alone decides.
No kernel may reach another device: no remote copies, remote signals or barrier semaphores. Data moves between devices by JAX's collectives and lax.ppermute only.
A program may use at most 64 MiB of HBM per device.

v0:
```python
import jax
import jax.numpy as jnp
from jax import lax
from jax.sharding import PartitionSpec as P


def from_everyone(array, axis):
    copies = jnp.broadcast_to(array, (lax.axis_size(axis), *array.shape))
    return lax.all_to_all(copies, axis, split_axis=0, concat_axis=0, tiled=True)


def taken_together(array, axis):
    everything = from_everyone(array, axis)
    return jnp.sum(everything, axis=0)


def filled_up(lines, count):
    spare = -len(lines) % count
    return jnp.pad(lines, [(0, spare)] + [(0, 0)] * (lines.ndim - 1))


def in_order(blocks, dim):
    blocks = jnp.moveaxis(blocks, 0, dim)
    shape = blocks.shape
    return blocks.reshape(*shape[:dim], shape[dim] * shape[dim + 1], *shape[dim + 2 :])


def gather_directly(array, axis, dim):
    return in_order(from_everyone(array, axis), dim)


def cut_along(array, dim, count):
    shape = array.shape
    blocks = array.reshape(*shape[:dim], count, shape[dim] // count, *shape[dim + 1 :])
    return jnp.moveaxis(blocks, dim, 0)


def sent_and_summed(array, axis, dim):
    blocks = cut_along(array, dim, lax.axis_size(axis))
    arrived = lax.all_to_all(blocks, axis, split_axis=0, concat_axis=0, tiled=True)
    return arrived.sum(axis=0)


def nested_sum(array, axes):
    lines = array.reshape(-1, array.shape[-1])
    padded = filled_up(lines, lax.axis_size(axes))
    whole = gather_directly(sent_and_summed(padded, axes, 0), axes, 0)
    return lax.slice_in_dim(whole, 0, len(lines)).reshape(array.shape)


def product(left, right):
    return jnp.dot(left, right, precision=lax.Precision.HIGHEST, preferred_element_type=jnp.float32)


def local(rhs, factor, inverses):
    span_rows = inverses.shape[2]
    span_cols = factor.shape[1] // 2
    first_rhs = rhs[:span_rows]
    second_rhs = rhs[span_rows : 2 * span_rows]
    trailing = rhs[2 * span_rows :]
    first_sol = taken_together(product(inverses[0], first_rhs), "row")
    reduced = second_rhs - nested_sum(product(factor[:span_rows, :span_cols], first_sol), "col")
    carried = product(factor[span_rows:, :span_cols], first_sol)
    second_sol = taken_together(product(inverses[1], reduced), "row")
    last_term = product(factor[span_rows:, span_cols:], second_sol)
    remaining = trailing - nested_sum(carried + last_term, "col")
    return (jnp.concatenate([first_sol, second_sol], 0), remaining)


def solution(mesh):
    in_specs = (P("row", None), P("row", "col"), P(None, "col", "row"))
    out_specs = (P("col", None), P("row", None))
    return jax.shard_map(local, mesh=mesh, in_specs=in_specs, out_specs=out_specs, check_vma=False)
```

profile of v0, /device:TPU:1, one launch (start us, length us, event | category | flops | bytes accessed | tf_op | source)
XLA Modules:
  0.0 208.1 jit_solution(12579569407566234036)
XLA Ops:
  0.6 1.0 fusion.8
  1.7 0.0 copy-start
  1.7 0.0 copy-start.2
  1.8 16.7 %all_to_all.30 = f32[16,64,128]{2,1,0:T(8,128)S(1)} all-to-all(f32[16,64,128]{2,1,0:T(8,128)S(1)} %broadcast_in_dim.12), channel_id=1, replica_groups=mesh['row'=16,'col'=32] {'row'}, dimensions={0} | all-to-all | bytes 1048576 | tf_op jit(solution)/shard_map/all_to_all | solution.py:9
  18.5 0.0 copy-done
  18.5 0.2 fusion.5
  18.7 31.3 %all_to_all.31 = f32[32,4,128]{2,1,0:T(4,128)S(1)} all-to-all(f32[32,4,128]{2,1,0:T(4,128)S(1)} %bitcast.22), channel_id=1, replica_groups=mesh['row'=16,'col'=32] {'col'}, dimensions={0} | all-to-all | bytes 131072 | tf_op jit(solution)/shard_map/all_to_all | solution.py:40
  50.1 17.3 %all_to_all.32 = f32[32,4,128]{2,1,0:T(4,128)S(1)} all-to-all(f32[32,4,128]{2,1,0:T(4,128)S(1)} %broadcast_in_dim.13), channel_id=1, replica_groups=mesh['row'=16,'col'=32] {'col'}, dimensions={0} | all-to-all | bytes 131072 | tf_op jit(solution)/shard_map/all_to_all | solution.py:9
  67.4 0.0 copy-done.2
  67.4 1.0 convolution_bitcast_fusion
  68.4 0.8 broadcast_in_dim.14
  69.3 3.6 %all-to-all-start.3 = ((f32[16,64,128]{2,1,0:T(8,128)}), f32[16,64,128]{2,1,0:T(8,128)S(1)}, u32[]{:S(2)}, u32[]{:S(2)}) async-start(f32[16,64,128]{2,1,0:T(8,128)} %broadcast_in_dim.14), calls=%async_computation.3 | async-start | bytes 1048576 | tf_op jit(solution)/shard_map/all_to_all | solution.py:9
  72.9 1.1 fusion.2
  74.0 8.0 %all-to-all-done.3 = f32[16,64,128]{2,1,0:T(8,128)S(1)} async-done(((f32[16,64,128]{2,1,0:T(8,128)}), f32[16,64,128]{2,1,0:T(8,128)S(1)}, u32[]{:S(2)}, u32[]{:S(2)}) %all-to-all-start.3) | async-done | bytes 524320 | tf_op jit(solution)/shard_map/all_to_all | solution.py:9
  81.9 1.4 fusion
  83.3 0.3 copy.6
  83.7 62.1 %all_to_all.33 = f32[32,64,128]{2,1,0:T(8,128)S(1)} all-to-all(f32[32,64,128]{2,1,0:T(8,128)S(1)} %bitcast.20), channel_id=1, replica_groups=mesh['row'=16,'col'=32] {'col'}, dimensions={0} | all-to-all | bytes 2097152 | tf_op jit(solution)/shard_map/all_to_all | solution.py:40
  145.8 0.1 reduce_sum.39
  145.9 1.1 broadcast_in_dim.15
  146.9 4.2 %all-to-all-start.5 = ((f32[32,64,128]{2,1,0:T(8,128)}), f32[32,64,128]{2,1,0:T(8,128)S(1)}, u32[]{:S(2)}, u32[]{:S(2)}) async-start(f32[32,64,128]{2,1,0:T(8,128)} %broadcast_in_dim.15), calls=%async_computation.5 | async-start | bytes 2097152 | tf_op jit(solution)/shard_map/all_to_all | solution.py:9
  151.2 0.6 pad_maximum_fusion
  151.8 55.2 %all-to-all-done.5 = f32[32,64,128]{2,1,0:T(8,128)S(1)} async-done(((f32[32,64,128]{2,1,0:T(8,128)}), f32[32,64,128]{2,1,0:T(8,128)S(1)}, u32[]{:S(2)}, u32[]{:S(2)}) %all-to-all-start.5) | async-done | bytes 1048608 | tf_op jit(solution)/shard_map/all_to_all | solution.py:9
  207.0 0.0 copy-done.1
  207.0 1.1 bitcast_subtract_fusion
  (6 shorter events, 0.2 us)
Async XLA Ops:
  1.7 16.8 %copy-start = (f32[2176,128]{1,0:T(8,128)S(1)}, f32[2176,128]{1,0:T(8,128)}, u32[]{:S(2)}) copy-start(f32[2176,128]{1,0:T(8,128)} %param.4) | copy-start | bytes 3342340
  1.7 65.7 %copy-start.2 = (f32[2,64,128]{2,1,0:T(8,128)S(1)}, f32[2,64,128]{2,1,0:T(8,128)}, u32[]{:S(2)}) copy-start(f32[2,64,128]{2,1,0:T(8,128)} %param.5) | copy-start | bytes 196612
  69.3 12.6 %all-to-all-start.3 = ((f32[16,64,128]{2,1,0:T(8,128)}), f32[16,64,128]{2,1,0:T(8,128)S(1)}, u32[]{:S(2)}, u32[]{:S(2)}) async-start(f32[16,64,128]{2,1,0:T(8,128)} %broadcast_in_dim.14), calls=%async_computation.3 | async-start | bytes 1048576 | tf_op jit(solution)/shard_map/all_to_all | solution.py:9
  146.9 60.0 %copy-start.1 = (f32[2304,128]{1,0:T(8,128)S(1)}, f32[2304,128]{1,0:T(8,128)}, u32[]{:S(2)}) copy-start(f32[2304,128]{1,0:T(8,128)} %param.3) | copy-start | bytes 3538948
  146.9 60.0 %all-to-all-start.5 = ((f32[32,64,128]{2,1,0:T(8,128)}), f32[32,64,128]{2,1,0:T(8,128)S(1)}, u32[]{:S(2)}, u32[]{:S(2)}) async-start(f32[32,64,128]{2,1,0:T(8,128)} %broadcast_in_dim.15), calls=%async_computation.5 | async-start | bytes 2097152 | tf_op jit(solution)/shard_map/all_to_all | solution.py:9
where the time goes:
time: 209 us; the launch traced here: 208 us
  blocking collectives  127 us (61%)
  waiting for transfers between devices  63.1 us (30%)
  starting transfers between devices  7.79 us (4%)
  matrix products  4.74 us (2%)
  local copies, waits for them, and re-layouts  2.33 us (1%)
    all_to_all x2, blocking collectives, sent_and_summed(): lax.all_to_all(blocks, axis, split_axis=0, concat_axis=0, tiled=True)  93.5 us
    all_to_all x2, waiting for transfers between devices, from_everyone(): return lax.all_to_all(copies, axis, split_axis=0, concat_axis=0, tiled=True)  63.1 us
    all_to_all x2, blocking collectives, from_everyone(): return lax.all_to_all(copies, axis, split_axis=0, concat_axis=0, tiled=True)  34 us
    all_to_all x2, starting transfers between devices, from_everyone(): return lax.all_to_all(copies, axis, split_axis=0, concat_axis=0, tiled=True)  7.79 us
    dot_general x5, matrix products, product(): jnp.dot(left, right, precision=lax.Precision.HIGHEST, preferred_element_t...  4.74 us
  transfers between devices with their start and end apart: 2, of which 2 were waited for; matrix products, arithmetic and copies ran while one was open for 1% of the time, Pallas kernels for 0%

commit v1 on v0

v1 whole, which is shorter than its diff:
```python
import jax
import jax.numpy as jnp
from jax import lax
from jax.sharding import Mesh
from jax.sharding import PartitionSpec as P

ROW = ("x", "y")
COL = ("z", "core")


def exchanged(blocks, axis):
    return lax.all_to_all(blocks, axis, split_axis=0, concat_axis=0, tiled=True)


def from_everyone(array, axis):
    return exchanged(jnp.broadcast_to(array, (lax.axis_size(axis), *array.shape)), axis)


def taken_together(array, axis):
    return jnp.sum(from_everyone(array, axis), axis=0)


def my_sum(array, axis):
    count = lax.axis_size(axis)
    blocks = array.reshape(count, array.shape[0] // count, *array.shape[1:])
    return jnp.sum(exchanged(blocks, axis), axis=0)


def gathered(array, axis):
    blocks = from_everyone(array, axis)
    return blocks.reshape(-1, *array.shape[1:])


def product(left, right):
    return jnp.dot(left, right, precision=lax.Precision.HIGHEST, preferred_element_type=jnp.float32)


def local(rhs, factor, inverses):
    span_rows = inverses.shape[2]
    span_cols = factor.shape[1] // 2
    first_rhs = rhs[:span_rows]
    second_rhs = rhs[span_rows : 2 * span_rows]
    trailing = rhs[2 * span_rows :]
    first_sol = taken_together(product(inverses[0], first_rhs), ROW)
    coupled = gathered(my_sum(product(factor[:span_rows, :span_cols], first_sol), COL), COL)
    carried = product(factor[span_rows:, :span_cols], first_sol)
    second_sol = taken_together(product(inverses[1], second_rhs - coupled), ROW)
    terms = carried + product(factor[span_rows:, span_cols:], second_sol)
    terms = my_sum(my_sum(terms, "core"), "z")
    rows = terms.shape[0]
    start = (lax.axis_index("core") * lax.axis_size("z") + lax.axis_index("z")) * rows
    mine = lax.dynamic_slice_in_dim(trailing, start, rows) - terms
    remaining = gathered(gathered(mine, "z"), "core")
    return (jnp.concatenate([first_sol, second_sol], 0), remaining)


def solution(mesh):
    rows, cols = mesh.devices.shape
    shape = (4, rows // 4, cols // 2, 2)
    torus = Mesh(mesh.devices.reshape(shape), (*ROW, *COL))
    in_specs = (P(ROW, None), P(ROW, COL), P(None, COL, ROW))
    out_specs = (P(COL, None), P(ROW, None))
    return jax.shard_map(local, mesh=torus, in_specs=in_specs, out_specs=out_specs, check_vma=False)
```

time: 209 us -> 167 us (0.80)
  blocking collectives: 127 us -> 84.2 us
  starting transfers between devices: 7.79 us -> 19 us
  waiting for transfers between devices: 63.1 us -> 53.8 us
    all_to_all x4 -> x5, blocking collectives: 127 us -> 84.2 us  [exchanged(): return lax.all_to_all(blocks, axis, split_axis=0, concat_axis=0, tiled=True)]
    all_to_all x2 -> x3, starting transfers between devices: 7.79 us -> 19 us  [exchanged(): return lax.all_to_all(blocks, axis, split_axis=0, concat_axis=0, tiled=True)]
    all_to_all x2 -> x3, waiting for transfers between devices: 63.1 us -> 53.8 us  [exchanged(): return lax.all_to_all(blocks, axis, split_axis=0, concat_axis=0, tiled=True)]
  transfers between devices with their start and end apart: 2 -> 3, of which waited for: 2 -> 3; matrix products, arithmetic and copies ran while one was open for 1% -> 1% of each run, Pallas kernels for 0% -> 0%
where the time goes in v1:
time: 167 us
  blocking collectives  84.2 us (50%)
  waiting for transfers between devices  53.8 us (32%)
  starting transfers between devices  19 us (11%)
  matrix products  3.91 us (2%)
  local copies, waits for them, and re-layouts  3.91 us (2%)
    all_to_all x5, blocking collectives, exchanged(): return lax.all_to_all(blocks, axis, split_axis=0, concat_axis=0, tiled=True)  84.2 us
    all_to_all x3, waiting for transfers between devices, exchanged(): return lax.all_to_all(blocks, axis, split_axis=0, concat_axis=0, tiled=True)  53.8 us
    all_to_all x3, starting transfers between devices, exchanged(): return lax.all_to_all(blocks, axis, split_axis=0, concat_axis=0, tiled=True)  19 us
    dot_general x5, matrix products, product(): jnp.dot(left, right, precision=lax.Precision.HIGHEST, preferred_element_t...  3.91 us
  transfers between devices with their start and end apart: 3, of which 3 were waited for; matrix products, arithmetic and copies ran while one was open for 1% of the time, Pallas kernels for 0%

profile of v1, /device:TPU:1, one launch (start us, length us, event | category | flops | bytes accessed | tf_op | source)
XLA Modules:
  0.0 166.5 jit_solution(5045034389591280727)
XLA Ops:
  0.6 1.0 fusion.7
  1.8 16.7 %all_to_all.40 = f32[16,64,128]{2,1,0:T(8,128)S(1)} all-to-all(f32[16,64,128]{2,1,0:T(8,128)S(1)} %broadcast_in_dim.15), channel_id=1, replica_groups=mesh['x'=4,'y'=4,'z'=16,'core'=2] {'x','y'}, dimensions={0} | all-to-all | bytes 1048576 | tf_op jit(solution)/shard_map/all_to_all | solution.py:12
  18.5 0.2 fusion.4
  18.7 31.3 %all_to_all.41 = f32[32,4,128]{2,1,0:T(4,128)S(1)} all-to-all(f32[32,4,128]{2,1,0:T(4,128)S(1)} %bitcast.28), channel_id=1, replica_groups=mesh['x'=4,'y'=4,'z'=16,'core'=2] {'z','core'}, dimensions={0} | all-to-all | bytes 131072 | tf_op jit(solution)/shard_map/all_to_all | solution.py:12
  50.1 17.3 %all_to_all.42 = f32[32,4,128]{2,1,0:T(4,128)S(1)} all-to-all(f32[32,4,128]{2,1,0:T(4,128)S(1)} %broadcast_in_dim.16), channel_id=1, replica_groups=mesh['x'=4,'y'=4,'z'=16,'core'=2] {'z','core'}, dimensions={0} | all-to-all | bytes 131072 | tf_op jit(solution)/shard_map/all_to_all | solution.py:12
  67.4 0.2 convolution_bitcast_fusion
  67.6 0.8 broadcast_in_dim.17
  68.5 3.6 %all-to-all-start.3 = ((f32[16,64,128]{2,1,0:T(8,128)}), f32[16,64,128]{2,1,0:T(8,128)S(1)}, u32[]{:S(2)}, u32[]{:S(2)}) async-start(f32[16,64,128]{2,1,0:T(8,128)} %broadcast_in_dim.17), calls=%async_computation.3 | async-start | bytes 1048576 | tf_op jit(solution)/shard_map/all_to_all | solution.py:12
  72.0 1.1 fusion.1
  73.1 7.9 %all-to-all-done.3 = f32[16,64,128]{2,1,0:T(8,128)S(1)} async-done(((f32[16,64,128]{2,1,0:T(8,128)}), f32[16,64,128]{2,1,0:T(8,128)S(1)}, u32[]{:S(2)}, u32[]{:S(2)}) %all-to-all-start.3) | async-done | bytes 524320 | tf_op jit(solution)/shard_map/all_to_all | solution.py:12
  81.1 1.4 convolution_add_fusion
  82.5 0.1 copy.16
  82.6 7.6 %all_to_all.43 = f32[2,1024,128]{1,2,0:T(8,128)S(1)} all-to-all(f32[2,1024,128]{1,2,0:T(8,128)S(1)} %bitcast.24), channel_id=1, replica_groups=mesh['x'=4,'y'=4,'z'=16,'core'=2] {'core'}, dimensions={0} | all-to-all | bytes 2097152 | tf_op jit(solution)/shard_map/all_to_all | solution.py:12
  90.2 0.1 reduce_sum.48
  90.3 1.0 copy.12
  91.3 3.6 %all-to-all-start.5 = ((f32[16,64,128]{2,1,0:T(8,128)}), f32[16,64,128]{2,1,0:T(8,128)S(1)}, u32[]{:S(2)}, u32[]{:S(2)}) async-start(f32[16,64,128]{2,1,0:T(8,128)} %bitcast.7), calls=%async_computation.5 | async-start | bytes 1048576 | tf_op jit(solution)/shard_map/all_to_all | solution.py:12
  94.9 23.7 %all-to-all-done.5 = f32[16,64,128]{2,1,0:T(8,128)S(1)} async-done(((f32[16,64,128]{2,1,0:T(8,128)}), f32[16,64,128]{2,1,0:T(8,128)S(1)}, u32[]{:S(2)}, u32[]{:S(2)}) %all-to-all-start.5) | async-done | bytes 524320 | tf_op jit(solution)/shard_map/all_to_all | solution.py:12
  118.6 0.8 broadcast_in_dim.18
  119.5 11.8 %all-to-all-start.6 = ((f32[16,64,128]{2,1,0:T(8,128)}), f32[16,64,128]{2,1,0:T(8,128)S(1)}, u32[]{:S(2)}, u32[]{:S(2)}) async-start(f32[16,64,128]{2,1,0:T(8,128)} %broadcast_in_dim.18), calls=%async_computation.6 | async-start | bytes 1048576 | tf_op jit(solution)/shard_map/all_to_all | solution.py:12
  131.3 0.6 pad_maximum_fusion
  131.9 22.2 %all-to-all-done.6 = f32[16,64,128]{2,1,0:T(8,128)S(1)} async-done(((f32[16,64,128]{2,1,0:T(8,128)}), f32[16,64,128]{2,1,0:T(8,128)S(1)}, u32[]{:S(2)}, u32[]{:S(2)}) %all-to-all-start.6) | async-done | bytes 524320 | tf_op jit(solution)/shard_map/all_to_all | solution.py:12
  154.1 0.1 broadcast_in_dim.19
  154.2 11.3 %all_to_all.44 = f32[2,1024,128]{2,1,0:T(8,128)S(1)} all-to-all(f32[2,1024,128]{2,1,0:T(8,128)S(1)} %broadcast_in_dim.19), channel_id=1, replica_groups=mesh['x'=4,'y'=4,'z'=16,'core'=2] {'core'}, dimensions={0} | all-to-all | bytes 2097152 | tf_op jit(solution)/shard_map/all_to_all | solution.py:12
  165.5 1.0 copy.18
  (15 shorter events, 0.2 us)
Async XLA Ops:
  1.7 16.9 %copy-start = (f32[2176,128]{1,0:T(8,128)S(1)}, f32[2176,128]{1,0:T(8,128)}, u32[]{:S(2)}) copy-start(f32[2176,128]{1,0:T(8,128)} %param.4) | copy-start | bytes 3342340
  1.7 65.7 %copy-start.1 = (f32[2304,128]{1,0:T(8,128)S(1)}, f32[2304,128]{1,0:T(8,128)}, u32[]{:S(2)}) copy-start(f32[2304,128]{1,0:T(8,128)} %param.3) | copy-start | bytes 3538948
  1.8 65.7 %copy-start.2 = (f32[2,64,128]{2,1,0:T(8,128)S(1)}, f32[2,64,128]{2,1,0:T(8,128)}, u32[]{:S(2)}) copy-start(f32[2,64,128]{2,1,0:T(8,128)} %param.5) | copy-start | bytes 196612
  68.5 12.6 %all-to-all-start.3 = ((f32[16,64,128]{2,1,0:T(8,128)}), f32[16,64,128]{2,1,0:T(8,128)S(1)}, u32[]{:S(2)}, u32[]{:S(2)}) async-start(f32[16,64,128]{2,1,0:T(8,128)} %broadcast_in_dim.17), calls=%async_computation.3 | async-start | bytes 1048576 | tf_op jit(solution)/shard_map/all_to_all | solution.py:12
  91.3 27.3 %all-to-all-start.5 = ((f32[16,64,128]{2,1,0:T(8,128)}), f32[16,64,128]{2,1,0:T(8,128)S(1)}, u32[]{:S(2)}, u32[]{:S(2)}) async-start(f32[16,64,128]{2,1,0:T(8,128)} %bitcast.7), calls=%async_computation.5 | async-start | bytes 1048576 | tf_op jit(solution)/shard_map/all_to_all | solution.py:12
  94.9 23.7 %slice-start = ((f32[2304,128]{1,0:T(8,128)}), f32[2048,128]{1,0:T(8,128)S(1)}, s32[]{:S(2)}) async-start(f32[2304,128]{1,0:T(8,128)} %param.3), calls=%async_computation.8 | async-start | bytes 2097152 | tf_op jit(solution)/shard_map/slice | solution.py:43
  119.5 34.7 %all-to-all-start.6 = ((f32[16,64,128]{2,1,0:T(8,128)}), f32[16,64,128]{2,1,0:T(8,128)S(1)}, u32[]{:S(2)}, u32[]{:S(2)}) async-start(f32[16,64,128]{2,1,0:T(8,128)} %broadcast_in_dim.18), calls=%async_computation.6 | async-start | bytes 1048576 | tf_op jit(solution)/shard_map/all_to_all | solution.py:12

commit v2 on v1

--- a/solution.py
+++ b/solution.py
@@ -40,18 +40,23 @@
     span_cols = factor.shape[1] // 2
     first_rhs = rhs[:span_rows]
     second_rhs = rhs[span_rows : 2 * span_rows]
-    trailing = rhs[2 * span_rows :]
-    first_sol = taken_together(product(inverses[0], first_rhs), ROW)
-    coupled = gathered(my_sum(product(factor[:span_rows, :span_cols], first_sol), COL), COL)
-    carried = product(factor[span_rows:, :span_cols], first_sol)
-    second_sol = taken_together(product(inverses[1], second_rhs - coupled), ROW)
-    terms = carried + product(factor[span_rows:, span_cols:], second_sol)
+    rows = (rhs.shape[0] - 2 * span_rows) // (lax.axis_size("z") * lax.axis_size("core"))
+    place = lax.axis_index("core") * lax.axis_size("z") + lax.axis_index("z")
+    trailing = lax.dynamic_slice_in_dim(rhs, 2 * span_rows + place * rows, rows)
+    first_part = product(inverses[0], first_rhs)
+    coupling = factor[:span_rows, :span_cols]
+    first_part, trailing, second_rhs, second_inverse, coupling = lax.optimization_barrier(
+        (first_part, trailing, second_rhs, inverses[1], coupling)
+    )
+    first_sol = taken_together(first_part, ROW)
+    coupled = gathered(my_sum(product(coupling, first_sol), COL), COL)
+    second_sol = taken_together(product(second_inverse, second_rhs - coupled), ROW)
+    both = jnp.concatenate([first_sol, second_sol], 0)
+    both, terms = lax.optimization_barrier((both, product(factor[span_rows:], both)))
     terms = my_sum(my_sum(terms, "core"), "z")
-    rows = terms.shape[0]
-    start = (lax.axis_index("core") * lax.axis_size("z") + lax.axis_index("z")) * rows
-    mine = lax.dynamic_slice_in_dim(trailing, start, rows) - terms
-    remaining = gathered(gathered(mine, "z"), "core")
-    return (jnp.concatenate([first_sol, second_sol], 0), remaining)
+    remaining = gathered(gathered(trailing - terms, "z"), "core")
+    both, remaining = lax.optimization_barrier((both, remaining))
+    return (both, remaining)
 
 
 def solution(mesh):

time: 167 us -> 166 us (level)
  blocking collectives: 84.2 us -> 157 us
  waiting for transfers between devices: 53.8 us -> 0 us
  starting transfers between devices: 19 us -> 0 us
    all_to_all x5 -> x8, blocking collectives: 84.2 us -> 157 us  [exchanged(): return lax.all_to_all(blocks, axis, split_axis=0, concat_axis=0, tiled=True)]
    all_to_all x3 -> x0, waiting for transfers between devices: 53.8 us -> none  [exchanged(): return lax.all_to_all(blocks, axis, split_axis=0, concat_axis=0, tiled=True)]
    all_to_all x3 -> x0, starting transfers between devices: 19 us -> none  [exchanged(): return lax.all_to_all(blocks, axis, split_axis=0, concat_axis=0, tiled=True)]
    dot_general x5 -> x4, matrix products: 3.91 us -> 2.5 us  [product(): jnp.dot(left, right, precision=lax.Precision.HIGHEST, preferred_element_t...]
  transfers between devices with their start and end apart: 3 -> 0, of which waited for: 3 -> 0; matrix products, arithmetic and copies ran while one was open for 1% -> 0% of each run, Pallas kernels for 0% -> 0%
where the time goes in v2:
time: 166 us; the launch traced here: 165 us
  blocking collectives  157 us (95%)
  local copies, waits for them, and re-layouts  3.9 us (2%)
  matrix products  2.5 us (2%)
    all_to_all x8, blocking collectives, exchanged(): return lax.all_to_all(blocks, axis, split_axis=0, concat_axis=0, tiled=True)  157 us

profile of v2, /device:TPU:1, one launch (start us, length us, event | category | flops | bytes accessed | tf_op | source)
XLA Modules:
  0.0 165.4 jit_solution(14931471055741891940)
XLA Ops:
  0.6 0.8 slice_bitcast_fusion
  1.4 1.0 fusion.5
  2.5 0.8 constant_dynamic-slice_fusion
  3.2 0.8 slice.22
  4.1 0.0 slice-start
  4.1 16.7 %all_to_all.40 = f32[16,64,128]{2,1,0:T(8,128)S(1)} all-to-all(f32[16,64,128]{2,1,0:T(8,128)S(1)} %broadcast_in_dim.15), channel_id=1, replica_groups=mesh['x'=4,'y'=4,'z'=16,'core'=2] {'x','y'}, dimensions={0} | all-to-all | bytes 1048576 | tf_op jit(solution)/shard_map/all_to_all | solution.py:12
  20.9 0.2 fusion.1
  21.2 31.3 %all_to_all.41 = f32[32,4,128]{2,1,0:T(4,128)S(1)} all-to-all(f32[32,4,128]{2,1,0:T(4,128)S(1)} %copy.16), channel_id=1, replica_groups=mesh['x'=4,'y'=4,'z'=16,'core'=2] {'z','core'}, dimensions={0} | all-to-all | bytes 131072 | tf_op jit(solution)/shard_map/all_to_all | solution.py:12
  52.6 17.3 %all_to_all.42 = f32[32,4,128]{2,1,0:T(4,128)S(1)} all-to-all(f32[32,4,128]{2,1,0:T(4,128)S(1)} %broadcast_in_dim.16), channel_id=1, replica_groups=mesh['x'=4,'y'=4,'z'=16,'core'=2] {'z','core'}, dimensions={0} | all-to-all | bytes 131072 | tf_op jit(solution)/shard_map/all_to_all | solution.py:12
  69.8 0.2 fusion.3
  70.0 0.0 copy-start
  70.1 12.4 %all_to_all.43 = f32[16,64,128]{2,1,0:T(8,128)S(1)} all-to-all(f32[16,64,128]{2,1,0:T(8,128)S(1)} %broadcast_in_dim.17), channel_id=1, replica_groups=mesh['x'=4,'y'=4,'z'=16,'core'=2] {'x','y'}, dimensions={0} | all-to-all | bytes 1048576 | tf_op jit(solution)/shard_map/all_to_all | solution.py:12
  82.5 0.6 pad_maximum_fusion
  83.1 0.0 copy-done
  83.1 1.1 convolution_bitcast_fusion
  84.2 0.1 copy.25
  84.3 7.4 %all_to_all.44 = f32[2,1024,128]{1,2,0:T(8,128)S(1)} all-to-all(f32[2,1024,128]{1,2,0:T(8,128)S(1)} %bitcast.21), channel_id=1, replica_groups=mesh['x'=4,'y'=4,'z'=16,'core'=2] {'core'}, dimensions={0} | all-to-all | bytes 2097152 | tf_op jit(solution)/shard_map/all_to_all | solution.py:12
  91.7 0.1 reduce_sum.48
  91.8 0.2 copy.19
  92.0 25.4 %all_to_all.45 = f32[16,64,128]{2,1,0:T(8,128)S(1)} all-to-all(f32[16,64,128]{2,1,0:T(8,128)S(1)} %bitcast.24), channel_id=1, replica_groups=mesh['x'=4,'y'=4,'z'=16,'core'=2] {'z'}, dimensions={0} | all-to-all | bytes 1048576 | tf_op jit(solution)/shard_map/all_to_all | solution.py:12
  117.6 35.5 %all_to_all.46 = f32[16,64,128]{2,1,0:T(8,128)S(1)} all-to-all(f32[16,64,128]{2,1,0:T(8,128)S(1)} %broadcast_in_dim.18), channel_id=1, replica_groups=mesh['x'=4,'y'=4,'z'=16,'core'=2] {'z'}, dimensions={0} | all-to-all | bytes 1048576 | tf_op jit(solution)/shard_map/all_to_all | solution.py:12
  153.0 0.1 broadcast_in_dim.19
  153.1 11.3 %all_to_all.47 = f32[2,1024,128]{2,1,0:T(8,128)S(1)} all-to-all(f32[2,1024,128]{2,1,0:T(8,128)S(1)} %broadcast_in_dim.19), channel_id=1, replica_groups=mesh['x'=4,'y'=4,'z'=16,'core'=2] {'core'}, dimensions={0} | all-to-all | bytes 2097152 | tf_op jit(solution)/shard_map/all_to_all | solution.py:12
  164.4 1.0 copy.27
  (11 shorter events, 0.3 us)
Async XLA Ops:
  4.1 65.7 %slice-start = ((f32[2304,128]{1,0:T(8,128)}), f32[128,128]{1,0:T(8,128)S(1)}, s32[]{:S(2)}) async-start(f32[2304,128]{1,0:T(8,128)} %param.3), calls=%async_computation.8 | async-start | bytes 131072 | tf_op jit(solution)/shard_map/slice | solution.py:42
  70.0 13.1 %copy-start = (f32[2176,128]{1,0:T(8,128)S(1)}, f32[2176,128]{1,0:T(8,128)}, u32[]{:S(2)}) copy-start(f32[2176,128]{1,0:T(8,128)} %param.4) | copy-start | bytes 3342340

commit v3 on v2

v3 whole, which is shorter than its diff:
```python
import jax
import jax.numpy as jnp
from jax import lax
from jax.sharding import Mesh
from jax.sharding import PartitionSpec as P

ROW = ("x", "y")
NEAR = ("zb", "zc", "core")
FAR = "za"
PARITY = ("za", "zb")
Z = ("za", "zb", "zc")
COL = (*Z, "core")
SWAP = [(0, 1), (1, 0)]


def exchanged(blocks, axis):
    return lax.all_to_all(blocks, axis, split_axis=0, concat_axis=0, tiled=True)


def from_everyone(array, axis):
    return exchanged(jnp.broadcast_to(array, (lax.axis_size(axis), *array.shape)), axis)


def taken_together(array, axis):
    return jnp.sum(from_everyone(array, axis), axis=0)


def my_sum(array, axis):
    count = lax.axis_size(axis)
    blocks = array.reshape(count, array.shape[0] // count, *array.shape[1:])
    return jnp.sum(exchanged(blocks, axis), axis=0)


def gathered(array, axis):
    return from_everyone(array, axis).reshape(-1, *array.shape[1:])


def product(left, right):
    return jnp.dot(left, right, precision=lax.Precision.HIGHEST, preferred_element_type=jnp.float32)


def part_of(array, start, rows):
    return lax.dynamic_slice(array, (start, jnp.uint32(0)), (rows, array.shape[1]))


def local(rhs, factor, inverses):
    span_rows = inverses.shape[2]
    span_cols = factor.shape[1] // 2
    first_rhs = rhs[:span_rows]
    second_rhs = rhs[span_rows : 2 * span_rows]
    spots = lax.axis_size(Z)
    rows = (rhs.shape[0] - 2 * span_rows) // (2 * spots)
    half = spots * rows
    core = lax.axis_index("core").astype(jnp.uint32)
    mine_at, other_at = core * half, (1 - core) * half
    place = 2 * span_rows + mine_at + lax.axis_index(Z).astype(jnp.uint32) * rows
    first_part = product(inverses[0], first_rhs)
    first_part, second_rhs, mine_at, other_at, place = lax.optimization_barrier(
        (first_part, second_rhs, mine_at, other_at, place)
    )

    first_sol = taken_together(first_part, ROW)
    coupled = lax.optimization_barrier(product(factor[:span_rows, :span_cols], first_sol))
    coupled = gathered(taken_together(my_sum(coupled, NEAR), FAR), NEAR)
    second_sol = taken_together(product(inverses[1], second_rhs - coupled), ROW)

    terms = product(factor[span_rows:], jnp.concatenate([first_sol, second_sol], 0))
    terms = terms.reshape(2, spots // 2, 2, rows, -1).swapaxes(1, 2).reshape(2 * half, -1)
    sent = part_of(terms, other_at, half)
    kept = part_of(terms, mine_at, half)
    sent, kept, first_sol, second_sol, rhs = lax.optimization_barrier((sent, kept, first_sol, second_sol, rhs))
    taken = lax.ppermute(sent, "core", SWAP)
    both = jnp.concatenate([first_sol, second_sol], 0)
    trailing = part_of(rhs, place, rows)
    taken, both, trailing = lax.optimization_barrier((taken, both, trailing))
    terms = my_sum(my_sum(kept + taken, "zc"), PARITY)

    mine = lax.all_gather(trailing - terms, Z, axis=0, tiled=True)
    other = lax.ppermute(mine, "core", SWAP)
    remaining = jnp.concatenate([mine, mine], 0)
    remaining = lax.dynamic_update_slice(remaining, other, (other_at, jnp.uint32(0)))
    return (both, remaining)


def solution(mesh):
    rows, cols = mesh.devices.shape
    shape = (4, rows // 4, cols // 8, 2, 2, 2)
    torus = Mesh(mesh.devices.reshape(shape), (*ROW, *COL))
    in_specs = (P(ROW, None), P(ROW, COL), P(None, COL, ROW))
    out_specs = (P(COL, None), P(ROW, None))
    return jax.shard_map(local, mesh=torus, in_specs=in_specs, out_specs=out_specs, check_vma=False)
```

time: 166 us -> 158 us (0.952)
  blocking collectives: 157 us -> 132 us
  starting transfers between devices: 0 us -> 14.2 us
  waiting for transfers between devices: 0 us -> 2.28 us
    all_to_all x8 -> x7, blocking collectives: 157 us -> 106 us  [exchanged(): return lax.all_to_all(blocks, axis, split_axis=0, concat_axis=0, tiled=True)]
    all_gather x0 -> x1, blocking collectives: none -> 25.9 us  [local(): mine = lax.all_gather(trailing - terms, Z, axis=0, tiled=True)]
    ppermute x0 -> x2, starting transfers between devices: none -> 14.2 us  [the longest x1 9.98 us: local(): other = lax.ppermute(mine, 'core', SWAP)]
    dynamic_update_slice x0 -> x1, local copies, waits for them, and re-layouts: none -> 2.79 us  [local(): lax.dynamic_update_slice(remaining, other, (other_at, jnp.uint32(0)))]
    ppermute x0 -> x2, waiting for transfers between devices: none -> 2.28 us  [the longest x1 1.44 us: local(): other = lax.ppermute(mine, 'core', SWAP)]
  transfers between devices with their start and end apart: 0 -> 2, of which waited for: 0 -> 2; matrix products, arithmetic and copies ran while one was open for 0% -> 0% of each run, Pallas kernels for 0% -> 0%
where the time goes in v3:
time: 158 us
  blocking collectives  132 us (84%)
  starting transfers between devices  14.2 us (9%)
  local copies, waits for them, and re-layouts  4.48 us (3%)
  matrix products  2.59 us (2%)
  waiting for transfers between devices  2.28 us (1%)
    all_to_all x7, blocking collectives, exchanged(): return lax.all_to_all(blocks, axis, split_axis=0, concat_axis=0, tiled=True)  106 us
    all_gather x1, blocking collectives, local(): mine = lax.all_gather(trailing - terms, Z, axis=0, tiled=True)  25.9 us
    ppermute x1, starting transfers between devices, local(): other = lax.ppermute(mine, 'core', SWAP)  9.98 us
    ppermute x1, starting transfers between devices, local(): taken = lax.ppermute(sent, 'core', SWAP)  4.27 us
  transfers between devices with their start and end apart: 2, of which 2 were waited for; matrix products, arithmetic and copies ran while one was open for 0% of the time, Pallas kernels for 0%

profile of v3, /device:TPU:1, one launch (start us, length us, event | category | flops | bytes accessed | tf_op | source)
XLA Modules:
  0.0 157.8 jit_solution(7130508781140567286)
XLA Ops:
  0.6 1.0 fusion.5
  1.8 16.7 %all_to_all.35 = f32[16,64,128]{2,1,0:T(8,128)S(1)} all-to-all(f32[16,64,128]{2,1,0:T(8,128)S(1)} %broadcast_in_dim.12), channel_id=1, replica_groups=mesh['x'=4,'y'=4,'za'=4,'zb'=2,'zc'=2,'core'=2] {'x','y'}, dimensions={0} | all-to-all | bytes 1048576 | tf_op jit(solution)/shard_map/all_to_all | solution.py:17
  18.6 0.3 convolution_bitcast_fusion.1
  18.9 0.1 copy.8
  19.0 14.0 %all_to_all.36 = f32[8,16,128]{2,1,0:T(8,128)S(1)} all-to-all(f32[8,16,128]{2,1,0:T(8,128)S(1)} %bitcast.27), channel_id=1, replica_groups=mesh['x'=4,'y'=4,'za'=4,'zb'=2,'zc'=2,'core'=2] {'zb','zc','core'}, dimensions={0} | all-to-all | bytes 131072 | tf_op jit(solution)/shard_map/all_to_all | solution.py:17
  33.0 23.4 %all_to_all.37 = f32[4,16,128]{2,1,0:T(8,128)S(1)} all-to-all(f32[4,16,128]{2,1,0:T(8,128)S(1)} %broadcast_in_dim.13), channel_id=1, replica_groups=mesh['x'=4,'y'=4,'za'=4,'zb'=2,'zc'=2,'core'=2] {'za'}, dimensions={0} | all-to-all | bytes 65536 | tf_op jit(solution)/shard_map/all_to_all | solution.py:17
  56.4 9.7 %all_to_all.38 = f32[8,16,128]{2,1,0:T(8,128)S(1)} all-to-all(f32[8,16,128]{2,1,0:T(8,128)S(1)} %broadcast_in_dim.14), channel_id=1, replica_groups=mesh['x'=4,'y'=4,'za'=4,'zb'=2,'zc'=2,'core'=2] {'zb','zc','core'}, dimensions={0} | all-to-all | bytes 131072 | tf_op jit(solution)/shard_map/all_to_all | solution.py:17
  66.2 0.2 convolution_bitcast_fusion.2
  66.4 13.2 %all_to_all.39 = f32[16,64,128]{2,1,0:T(8,128)S(1)} all-to-all(f32[16,64,128]{2,1,0:T(8,128)S(1)} %broadcast_in_dim.15), channel_id=1, replica_groups=mesh['x'=4,'y'=4,'za'=4,'zb'=2,'zc'=2,'core'=2] {'x','y'}, dimensions={0} | all-to-all | bytes 1048576 | tf_op jit(solution)/shard_map/all_to_all | solution.py:17
  79.7 1.1 convolution_bitcast_fusion
  80.8 0.3 copy.9
  81.1 0.1 copy.10
  81.2 0.1 constant_dynamic-slice_fusion.1
  81.3 4.3 %collective-permute-start = (f32[1024,128]{1,0:T(8,128)S(1)}, f32[1024,128]{1,0:T(8,128)S(1)}, u32[]{:S(2)}, u32[]{:S(2)}) collective-permute-start(f32[1024,128]{1,0:T(8,128)S(1)} %get-tuple-element.19), channel_id=1, source_target_pairs={{0,1},{1,0},{2,3},{3,2},{4,5},{5,4},{6,7},{7,6},{8,9},{9,8},{10,11... | collective-permute-start | bytes 1572872 | tf_op jit(solution)/shard_map/ppermute | solution.py:72
  85.6 0.6 pad_maximum_fusion.1
  86.2 0.8 collective-permute-done
  87.1 0.1 add.15
  87.2 10.1 %all_to_all.40 = f32[2,512,128]{2,1,0:T(8,128)S(1)} all-to-all(f32[2,512,128]{2,1,0:T(8,128)S(1)} %bitcast.25), channel_id=1, replica_groups=mesh['x'=4,'y'=4,'za'=4,'zb'=2,'zc'=2,'core'=2] {'zc'}, dimensions={0} | all-to-all | bytes 1048576 | tf_op jit(solution)/shard_map/all_to_all | solution.py:17
  97.3 19.2 %all_to_all.41 = f32[8,64,128]{2,1,0:T(8,128)S(1)} all-to-all(f32[8,64,128]{2,1,0:T(8,128)S(1)} %bitcast.26), channel_id=1, replica_groups=mesh['x'=4,'y'=4,'za'=4,'zb'=2,'zc'=2,'core'=2] {'za','zb'}, dimensions={0} | all-to-all | bytes 524288 | tf_op jit(solution)/shard_map/all_to_all | solution.py:17
  116.6 25.9 %all_gather.3 = f32[1024,128]{1,0:T(8,128)S(1)} all-gather(f32[64,128]{1,0:T(8,128)S(1)} %sub.11), channel_id=1, replica_groups=mesh['x'=4,'y'=4,'za'=4,'zb'=2,'zc'=2,'core'=2] {'za','zb','zc'}, dimensions={0}, use_global_device_ids=true | all-gather | bytes 557056 | tf_op jit(solution)/shard_map/all_gather | solution.py:78
  142.5 10.0 %collective-permute-start.1 = (f32[1024,128]{1,0:T(8,128)S(1)}, f32[1024,128]{1,0:T(8,128)S(1)}, u32[]{:S(2)}, u32[]{:S(2)}) collective-permute-start(f32[1024,128]{1,0:T(8,128)S(1)} %all_gather.3), channel_id=1, source_target_pairs={{0,1},{1,0},{2,3},{3,2},{4,5},{5,4},{6,7},{7,6},{8,9},{9,8},{10,11... | collective-permute-start | bytes 1572872 | tf_op jit(solution)/shard_map/ppermute | solution.py:79
  152.5 1.4 collective-permute-done.1
  154.0 2.8 %dynamic_update_slice.3 = f32[2048,128]{1,0:T(8,128)S(1)} dynamic-update-slice(f32[2048,128]{1,0:T(8,128)S(1)} %pad_maximum_fusion, f32[1024,128]{1,0:T(8,128)S(1)} %collective-permute-done.1, u32[]{:T(128)S(6)} %mul.16, u32[]{:T(128)} %constant.27.clone.1) | dynamic-update-slice | bytes 1048580 | tf_op jit(solution)/shard_map/dynamic_update_slice | solution.py:81
  156.8 1.0 copy-done.1
  (23 shorter events, 0.4 us)
Async XLA Ops:
  1.7 16.9 %copy-start = (f32[2176,128]{1,0:T(8,128)S(1)}, f32[2176,128]{1,0:T(8,128)}, u32[]{:S(2)}) copy-start(f32[2176,128]{1,0:T(8,128)} %param.4) | copy-start | bytes 3342340
  1.8 64.4 %slice-start = ((f32[2304,128]{1,0:T(8,128)}), f32[128,128]{1,0:T(8,128)S(1)}, s32[]{:S(2)}) async-start(f32[2304,128]{1,0:T(8,128)} %param.3), calls=%async_computation.7 | async-start | bytes 131072 | tf_op jit(solution)/shard_map/slice | solution.py:50
  1.8 64.4 %copy-start.3 = (f32[2,64,128]{2,1,0:T(8,128)S(1)}, f32[2,64,128]{2,1,0:T(8,128)}, u32[]{:S(2)}) copy-start(f32[2,64,128]{2,1,0:T(8,128)} %param.5) | copy-start | bytes 196612
  81.2 4.4 %copy-start.2 = (f32[2304,128]{1,0:T(8,128)S(1)}, f32[2304,128]{1,0:T(8,128)}, u32[]{:S(2)}) copy-start(f32[2304,128]{1,0:T(8,128)} %param.3) | copy-start | bytes 3538948
  81.3 5.8 %collective-permute-start = (f32[1024,128]{1,0:T(8,128)S(1)}, f32[1024,128]{1,0:T(8,128)S(1)}, u32[]{:S(2)}, u32[]{:S(2)}) collective-permute-start(f32[1024,128]{1,0:T(8,128)S(1)} %get-tuple-element.19), channel_id=1, source_target_pairs={{0,1},{1,0},{2,3},{3,2},{4,5},{5,4},{6,7},{7,6},{8,9},{9,8},{10,11... | collective-permute-start | bytes 1572872 | tf_op jit(solution)/shard_map/ppermute | solution.py:72
  142.5 11.5 %collective-permute-start.1 = (f32[1024,128]{1,0:T(8,128)S(1)}, f32[1024,128]{1,0:T(8,128)S(1)}, u32[]{:S(2)}, u32[]{:S(2)}) collective-permute-start(f32[1024,128]{1,0:T(8,128)S(1)} %all_gather.3), channel_id=1, source_target_pairs={{0,1},{1,0},{2,3},{3,2},{4,5},{5,4},{6,7},{7,6},{8,9},{9,8},{10,11... | collective-permute-start | bytes 1572872 | tf_op jit(solution)/shard_map/ppermute | solution.py:79
  156.8 1.0 copy-start.1

commit v4 on v3

--- a/solution.py
+++ b/solution.py
@@ -5,10 +5,8 @@
 from jax.sharding import PartitionSpec as P
 
 ROW = ("x", "y")
-NEAR = ("zb", "zc", "core")
-FAR = "za"
-PARITY = ("za", "zb")
-Z = ("za", "zb", "zc")
+NEAR = ("pair", "core")
+Z = ("parity", "pair")
 COL = (*Z, "core")
 SWAP = [(0, 1), (1, 0)]
 
@@ -52,39 +50,42 @@
     rows = (rhs.shape[0] - 2 * span_rows) // (2 * spots)
     half = spots * rows
     core = lax.axis_index("core").astype(jnp.uint32)
-    mine_at, other_at = core * half, (1 - core) * half
-    place = 2 * span_rows + mine_at + lax.axis_index(Z).astype(jnp.uint32) * rows
+    pair = lax.axis_index("pair").astype(jnp.uint32)
+    quarter = half // 2
+    place = 2 * span_rows + core * half + lax.axis_index(Z).astype(jnp.uint32) * rows
+    starts = (core * half, (1 - core) * half, pair * quarter, (1 - pair) * quarter, place)
     first_part = product(inverses[0], first_rhs)
-    first_part, second_rhs, mine_at, other_at, place = lax.optimization_barrier(
-        (first_part, second_rhs, mine_at, other_at, place)
-    )
+    first_part, second_rhs, starts = lax.optimization_barrier((first_part, second_rhs, starts))
+    half_kept, half_sent, quarter_kept, quarter_sent, place = starts
 
     first_sol = taken_together(first_part, ROW)
     coupled = lax.optimization_barrier(product(factor[:span_rows, :span_cols], first_sol))
-    coupled = gathered(taken_together(my_sum(coupled, NEAR), FAR), NEAR)
+    coupled = gathered(taken_together(my_sum(coupled, NEAR), "parity"), NEAR)
     second_sol = taken_together(product(inverses[1], second_rhs - coupled), ROW)
 
-    terms = product(factor[span_rows:], jnp.concatenate([first_sol, second_sol], 0))
+    both = lax.optimization_barrier(jnp.concatenate([first_sol, second_sol], 0))
+    terms = product(factor[span_rows:], both)
     terms = terms.reshape(2, spots // 2, 2, rows, -1).swapaxes(1, 2).reshape(2 * half, -1)
-    sent = part_of(terms, other_at, half)
-    kept = part_of(terms, mine_at, half)
-    sent, kept, first_sol, second_sol, rhs = lax.optimization_barrier((sent, kept, first_sol, second_sol, rhs))
+    sent, kept = part_of(terms, half_sent, half), part_of(terms, half_kept, half)
+    sent, kept, rhs = lax.optimization_barrier((sent, kept, rhs))
     taken = lax.ppermute(sent, "core", SWAP)
-    both = jnp.concatenate([first_sol, second_sol], 0)
     trailing = part_of(rhs, place, rows)
-    taken, both, trailing = lax.optimization_barrier((taken, both, trailing))
-    terms = my_sum(my_sum(kept + taken, "zc"), PARITY)
+    taken, trailing = lax.optimization_barrier((taken, trailing))
+    terms = kept + taken
+    sent, kept = part_of(terms, quarter_sent, quarter), part_of(terms, quarter_kept, quarter)
+    terms = my_sum(kept + lax.ppermute(sent, "pair", SWAP), "parity")
 
     mine = lax.all_gather(trailing - terms, Z, axis=0, tiled=True)
     other = lax.ppermute(mine, "core", SWAP)
-    remaining = jnp.concatenate([mine, mine], 0)
-    remaining = lax.dynamic_update_slice(remaining, other, (other_at, jnp.uint32(0)))
+    remaining = jnp.where(
+        lax.axis_index("core") == 0, jnp.concatenate([mine, other], 0), jnp.concatenate([other, mine], 0)
+    )
     return (both, remaining)
 
 
 def solution(mesh):
     rows, cols = mesh.devices.shape
-    shape = (4, rows // 4, cols // 8, 2, 2, 2)
+    shape = (4, rows // 4, cols // 4, 2, 2)
     torus = Mesh(mesh.devices.reshape(shape), (*ROW, *COL))
     in_specs = (P(ROW, None), P(ROW, COL), P(None, COL, ROW))
     out_specs = (P(COL, None), P(ROW, None))

time: 158 us -> 153 us (0.968)
  blocking collectives: 132 us -> 120 us
  waiting for transfers between devices: 2.28 us -> 10.5 us
  local copies, waits for them, and re-layouts: 4.48 us -> 0.75 us
  starting transfers between devices: 14.2 us -> 16.3 us
    all_to_all x7 -> x6, blocking collectives: 106 us -> 94.8 us  [exchanged(): return lax.all_to_all(blocks, axis, split_axis=0, concat_axis=0, tiled=True)]
    ppermute x0 -> x1, waiting for transfers between devices: none -> 7.49 us  [local(): terms = my_sum(kept + lax.ppermute(sent, 'pair', SWAP), 'parity')]
    dynamic_update_slice x1 -> x0, local copies, waits for them, and re-layouts: 2.79 us -> none  [local(): lax.dynamic_update_slice(remaining, other, (other_at, jnp.uint32(0)))]
    ppermute x0 -> x1, starting transfers between devices: none -> 1.92 us  [local(): terms = my_sum(kept + lax.ppermute(sent, 'pair', SWAP), 'parity')]
  transfers between devices with their start and end apart: 2 -> 3, of which waited for: 2 -> 3; matrix products, arithmetic and copies ran while one was open for 0% -> 0% of each run, Pallas kernels for 0% -> 0%
where the time goes in v4:
time: 153 us
  blocking collectives  120 us (78%)
  starting transfers between devices  16.3 us (11%)
  waiting for transfers between devices  10.5 us (7%)
  matrix products  2.58 us (2%)
    all_to_all x6, blocking collectives, exchanged(): return lax.all_to_all(blocks, axis, split_axis=0, concat_axis=0, tiled=True)  94.8 us
    all_gather x1, blocking collectives, local(): mine = lax.all_gather(trailing - terms, Z, axis=0, tiled=True)  25.4 us
    ppermute x1, starting transfers between devices, local(): other = lax.ppermute(mine, 'core', SWAP)  10.1 us
    ppermute x1, waiting for transfers between devices, local(): terms = my_sum(kept + lax.ppermute(sent, 'pair', SWAP), 'parity')  7.49 us
    ppermute x1, starting transfers between devices, local(): taken = lax.ppermute(sent, 'core', SWAP)  4.31 us
  transfers between devices with their start and end apart: 3, of which 3 were waited for; matrix products, arithmetic and copies ran while one was open for 0% of the time, Pallas kernels for 0%

profile of v4, /device:TPU:1, one launch (start us, length us, event | category | flops | bytes accessed | tf_op | source)
XLA Modules:
  0.0 152.6 jit_solution(7753135739127656672)
XLA Ops:
  0.6 1.0 fusion.2
  1.8 16.7 %all_to_all.30 = f32[16,64,128]{2,1,0:T(8,128)S(1)} all-to-all(f32[16,64,128]{2,1,0:T(8,128)S(1)} %broadcast_in_dim.12), channel_id=1, replica_groups=mesh['x'=4,'y'=4,'parity'=8,'pair'=2,'core'=2] {'x','y'}, dimensions={0} | all-to-all | bytes 1048576 | tf_op jit(solution)/shard_map/all_to_all | solution.py:15
  18.5 0.3 convolution_bitcast_fusion.1
  18.8 0.1 copy.8
  18.9 9.5 %all_to_all.31 = f32[4,32,128]{2,1,0:T(8,128)S(1)} all-to-all(f32[4,32,128]{2,1,0:T(8,128)S(1)} %bitcast.26), channel_id=1, replica_groups=mesh['x'=4,'y'=4,'parity'=8,'pair'=2,'core'=2] {'pair','core'}, dimensions={0} | all-to-all | bytes 131072 | tf_op jit(solution)/shard_map/all_to_all | solution.py:15
  28.4 27.4 %all_to_all.32 = f32[8,32,128]{2,1,0:T(8,128)S(1)} all-to-all(f32[8,32,128]{2,1,0:T(8,128)S(1)} %broadcast_in_dim.13), channel_id=1, replica_groups=mesh['x'=4,'y'=4,'parity'=8,'pair'=2,'core'=2] {'parity'}, dimensions={0} | all-to-all | bytes 262144 | tf_op jit(solution)/shard_map/all_to_all | solution.py:15
  55.9 8.4 %all_to_all.33 = f32[4,32,128]{2,1,0:T(8,128)S(1)} all-to-all(f32[4,32,128]{2,1,0:T(8,128)S(1)} %broadcast_in_dim.14), channel_id=1, replica_groups=mesh['x'=4,'y'=4,'parity'=8,'pair'=2,'core'=2] {'pair','core'}, dimensions={0} | all-to-all | bytes 131072 | tf_op jit(solution)/shard_map/all_to_all | solution.py:15
  64.3 0.2 convolution_bitcast_fusion.2
  64.6 13.2 %all_to_all.34 = f32[16,64,128]{2,1,0:T(8,128)S(1)} all-to-all(f32[16,64,128]{2,1,0:T(8,128)S(1)} %broadcast_in_dim.15), channel_id=1, replica_groups=mesh['x'=4,'y'=4,'parity'=8,'pair'=2,'core'=2] {'x','y'}, dimensions={0} | all-to-all | bytes 1048576 | tf_op jit(solution)/shard_map/all_to_all | solution.py:15
  77.8 0.0 copy-start.1
  77.8 1.1 convolution_bitcast_fusion
  78.9 0.3 copy.9
  79.3 0.1 copy.10
  79.4 0.1 constant_dynamic-slice_fusion.2
  79.5 4.3 %collective-permute-start = (f32[1024,128]{1,0:T(8,128)S(1)}, f32[1024,128]{1,0:T(8,128)S(1)}, u32[]{:S(2)}, u32[]{:S(2)}) collective-permute-start(f32[1024,128]{1,0:T(8,128)S(1)} %get-tuple-element.18), channel_id=1, source_target_pairs={{0,1},{1,0},{2,3},{3,2},{4,5},{5,4},{6,7},{7,6},{8,9},{9,8},{10,11... | collective-permute-start | bytes 1572872 | tf_op jit(solution)/shard_map/ppermute | solution.py:71
  83.8 1.5 collective-permute-done
  85.3 0.1 add.14
  85.4 1.9 %collective-permute-start.1 = (f32[512,128]{1,0:T(8,128)S(1)}, f32[512,128]{1,0:T(8,128)S(1)}, u32[]{:S(2)}, u32[]{:S(2)}) collective-permute-start(f32[512,128]{1,0:T(8,128)S(1)} %constant_dynamic-slice_fusion), channel_id=1, source_target_pairs={{0,2},{2,0},{1,3},{3,1},{4,6},{6,4},{5,7},{7,5},{8,10},{10,8},{9,1... | collective-permute-start | bytes 786440 | tf_op jit(solution)/shard_map/ppermute | solution.py:76
  87.3 7.5 %collective-permute-done.1 = f32[512,128]{1,0:T(8,128)S(1)} collective-permute-done((f32[512,128]{1,0:T(8,128)S(1)}, f32[512,128]{1,0:T(8,128)S(1)}, u32[]{:S(2)}, u32[]{:S(2)}) %collective-permute-start.1) | collective-permute-done | bytes 262176 | tf_op jit(solution)/shard_map/ppermute | solution.py:76
  94.9 19.6 %all_to_all.35 = f32[8,64,128]{2,1,0:T(8,128)S(1)} all-to-all(f32[8,64,128]{2,1,0:T(8,128)S(1)} %bitcast.25), channel_id=1, replica_groups=mesh['x'=4,'y'=4,'parity'=8,'pair'=2,'core'=2] {'parity'}, dimensions={0} | all-to-all | bytes 524288 | tf_op jit(solution)/shard_map/all_to_all | solution.py:15
  114.5 25.4 %all_gather.3 = f32[1024,128]{1,0:T(8,128)S(1)} all-gather(f32[64,128]{1,0:T(8,128)S(1)} %sub.15), channel_id=1, replica_groups=mesh['x'=4,'y'=4,'parity'=8,'pair'=2,'core'=2] {'parity','pair'}, dimensions={0}, use_global_device_ids=true | all-gather | bytes 557056 | tf_op jit(solution)/shard_map/all_gather | solution.py:78
  139.9 10.1 %collective-permute-start.2 = (f32[1024,128]{1,0:T(8,128)S(1)}, f32[1024,128]{1,0:T(8,128)S(1)}, u32[]{:S(2)}, u32[]{:S(2)}) collective-permute-start(f32[1024,128]{1,0:T(8,128)S(1)} %all_gather.3), channel_id=1, source_target_pairs={{0,1},{1,0},{2,3},{3,2},{4,5},{5,4},{6,7},{7,6},{8,9},{9,8},{10,11... | collective-permute-start | bytes 1572872 | tf_op jit(solution)/shard_map/ppermute | solution.py:79
  150.0 1.5 collective-permute-done.2
  151.5 1.1 maximum_select_fusion
  (24 shorter events, 0.3 us)
Async XLA Ops:
  1.7 16.8 %copy-start = (f32[2176,128]{1,0:T(8,128)S(1)}, f32[2176,128]{1,0:T(8,128)}, u32[]{:S(2)}) copy-start(f32[2176,128]{1,0:T(8,128)} %param.4) | copy-start | bytes 3342340
  18.5 45.8 %slice-start = ((f32[2304,128]{1,0:T(8,128)}), f32[128,128]{1,0:T(8,128)S(1)}, s32[]{:S(2)}) async-start(f32[2304,128]{1,0:T(8,128)} %param.3), calls=%async_computation.6 | async-start | bytes 131072 | tf_op jit(solution)/shard_map/slice | solution.py:48
  18.5 45.8 %copy-start.3 = (f32[2,64,128]{2,1,0:T(8,128)S(1)}, f32[2,64,128]{2,1,0:T(8,128)}, u32[]{:S(2)}) copy-start(f32[2,64,128]{2,1,0:T(8,128)} %param.5) | copy-start | bytes 196612
  77.8 1.4 copy-start.1
  79.3 4.4 %copy-start.2 = (f32[2304,128]{1,0:T(8,128)S(1)}, f32[2304,128]{1,0:T(8,128)}, u32[]{:S(2)}) copy-start(f32[2304,128]{1,0:T(8,128)} %param.3) | copy-start | bytes 3538948
  79.5 5.8 %collective-permute-start = (f32[1024,128]{1,0:T(8,128)S(1)}, f32[1024,128]{1,0:T(8,128)S(1)}, u32[]{:S(2)}, u32[]{:S(2)}) collective-permute-start(f32[1024,128]{1,0:T(8,128)S(1)} %get-tuple-element.18), channel_id=1, source_target_pairs={{0,1},{1,0},{2,3},{3,2},{4,5},{5,4},{6,7},{7,6},{8,9},{9,8},{10,11... | collective-permute-start | bytes 1572872 | tf_op jit(solution)/shard_map/ppermute | solution.py:71
  85.4 9.4 %collective-permute-start.1 = (f32[512,128]{1,0:T(8,128)S(1)}, f32[512,128]{1,0:T(8,128)S(1)}, u32[]{:S(2)}, u32[]{:S(2)}) collective-permute-start(f32[512,128]{1,0:T(8,128)S(1)} %constant_dynamic-slice_fusion), channel_id=1, source_target_pairs={{0,2},{2,0},{1,3},{3,1},{4,6},{6,4},{5,7},{7,5},{8,10},{10,8},{9,1... | collective-permute-start | bytes 786440 | tf_op jit(solution)/shard_map/ppermute | solution.py:76
  139.9 11.6 %collective-permute-start.2 = (f32[1024,128]{1,0:T(8,128)S(1)}, f32[1024,128]{1,0:T(8,128)S(1)}, u32[]{:S(2)}, u32[]{:S(2)}) collective-permute-start(f32[1024,128]{1,0:T(8,128)S(1)} %all_gather.3), channel_id=1, source_target_pairs={{0,1},{1,0},{2,3},{3,2},{4,5},{5,4},{6,7},{7,6},{8,9},{9,8},{10,11... | collective-permute-start | bytes 1572872 | tf_op jit(solution)/shard_map/ppermute | solution.py:79

commit v5 on v4

--- a/solution.py
+++ b/solution.py
@@ -38,7 +38,13 @@
 
 
 def part_of(array, start, rows):
-    return lax.dynamic_slice(array, (start, jnp.uint32(0)), (rows, array.shape[1]))
+    return lax.dynamic_slice(array, (start, 0), (rows, array.shape[1]), allow_negative_indices=False)
+
+
+def every_other(blocks, first, which):
+    sizes = (blocks.shape[0] - 1, 1, *blocks.shape[2:])
+    part = lax.dynamic_slice(blocks, (first, which, 0, 0), sizes, allow_negative_indices=False)
+    return part.reshape(-1, blocks.shape[-1])
 
 
 def local(rhs, factor, inverses):
@@ -48,32 +54,39 @@
     second_rhs = rhs[span_rows : 2 * span_rows]
     spots = lax.axis_size(Z)
     rows = (rhs.shape[0] - 2 * span_rows) // (2 * spots)
-    half = spots * rows
-    core = lax.axis_index("core").astype(jnp.uint32)
-    pair = lax.axis_index("pair").astype(jnp.uint32)
-    quarter = half // 2
-    place = 2 * span_rows + core * half + lax.axis_index(Z).astype(jnp.uint32) * rows
-    starts = (core * half, (1 - core) * half, pair * quarter, (1 - pair) * quarter, place)
+    half = spots * rows // 2
+    core = lax.axis_index("core")
+    pair = lax.axis_index("pair")
+    place = 2 * span_rows + (core * spots + lax.axis_index(Z)) * rows
+    starts = (core * half, (1 - core) * half, pair, 1 - pair, place, jnp.int32(1))
     first_part = product(inverses[0], first_rhs)
     first_part, second_rhs, starts = lax.optimization_barrier((first_part, second_rhs, starts))
-    half_kept, half_sent, quarter_kept, quarter_sent, place = starts
+    half_kept, half_sent, pair, other_pair, place, one = starts
 
     first_sol = taken_together(first_part, ROW)
     coupled = lax.optimization_barrier(product(factor[:span_rows, :span_cols], first_sol))
-    coupled = gathered(taken_together(my_sum(coupled, NEAR), "parity"), NEAR)
-    second_sol = taken_together(product(inverses[1], second_rhs - coupled), ROW)
+    coupled = my_sum(coupled, NEAR)
+    coupled, factor = lax.optimization_barrier((coupled, factor))
+    blocks = factor.reshape(-1, 2, span_rows // 2, factor.shape[1])
+    kept, sent = every_other(blocks, one, pair), every_other(blocks, one, other_pair)
+    sent, kept, coupled = lax.optimization_barrier((sent, kept, coupled))
+    came = lax.ppermute(sent, "pair", SWAP)
+    coupled = gathered(taken_together(coupled, "parity"), NEAR)
+    came, coupled = lax.optimization_barrier((came, coupled))
+    second_part = product(inverses[1], second_rhs - coupled)
+    second_sol = taken_together(second_part, ROW)
 
     both = lax.optimization_barrier(jnp.concatenate([first_sol, second_sol], 0))
-    terms = product(factor[span_rows:], both)
-    terms = terms.reshape(2, spots // 2, 2, rows, -1).swapaxes(1, 2).reshape(2 * half, -1)
+    theirs = lax.ppermute(both, "pair", SWAP)
+    terms = product(kept, both)
+    theirs, terms = lax.optimization_barrier((theirs, terms))
+    terms = terms + product(came, theirs)
     sent, kept = part_of(terms, half_sent, half), part_of(terms, half_kept, half)
     sent, kept, rhs = lax.optimization_barrier((sent, kept, rhs))
     taken = lax.ppermute(sent, "core", SWAP)
     trailing = part_of(rhs, place, rows)
     taken, trailing = lax.optimization_barrier((taken, trailing))
-    terms = kept + taken
-    sent, kept = part_of(terms, quarter_sent, quarter), part_of(terms, quarter_kept, quarter)
-    terms = my_sum(kept + lax.ppermute(sent, "pair", SWAP), "parity")
+    terms = my_sum(kept + taken, "parity")
 
     mine = lax.all_gather(trailing - terms, Z, axis=0, tiled=True)
     other = lax.ppermute(mine, "core", SWAP)

time: 153 us -> 156 us (1.020)
  blocking collectives: 120 us -> 86.8 us
  starting transfers between devices: 16.3 us -> 41.5 us
  waiting for transfers between devices: 10.5 us -> 20 us
    all_to_all x6 -> x4, blocking collectives: 94.8 us -> 62.9 us  [exchanged(): return lax.all_to_all(blocks, axis, split_axis=0, concat_axis=0, tiled=True)]
    all_to_all x0 -> x2, starting transfers between devices: none -> 21.2 us  [exchanged(): return lax.all_to_all(blocks, axis, split_axis=0, concat_axis=0, tiled=True)]
    all_to_all x0 -> x2, waiting for transfers between devices: none -> 14.9 us  [exchanged(): return lax.all_to_all(blocks, axis, split_axis=0, concat_axis=0, tiled=True)]
    ppermute x1 -> x2, waiting for transfers between devices: 7.49 us -> 2.51 us  [the longest x1 2.51 us: local(): theirs = lax.ppermute(both, 'pair', SWAP)]
    ppermute x1 -> x2, starting transfers between devices: 1.92 us -> 3.83 us  [the longest x1 1.92 us: local(): theirs = lax.ppermute(both, 'pair', SWAP)]
  transfers between devices with their start and end apart: 3 -> 6, of which waited for: 3 -> 5; matrix products, arithmetic and copies ran while one was open for 0% -> 1% of each run, Pallas kernels for 0% -> 0%
where the time goes in v5:
time: 156 us; the launch traced here: 155 us
  blocking collectives  86.8 us (56%)
  starting transfers between devices  41.5 us (27%)
  waiting for transfers between devices  20 us (13%)
  matrix products  2.72 us (2%)
  local copies, waits for them, and re-layouts  1.69 us (1%)
    all_to_all x4, blocking collectives, exchanged(): return lax.all_to_all(blocks, axis, split_axis=0, concat_axis=0, tiled=True)  62.9 us
    all_gather x1, blocking collectives, local(): mine = lax.all_gather(trailing - terms, Z, axis=0, tiled=True)  23.9 us
    all_to_all x2, starting transfers between devices, exchanged(): return lax.all_to_all(blocks, axis, split_axis=0, concat_axis=0, tiled=True)  21.2 us
    all_to_all x2, waiting for transfers between devices, exchanged(): return lax.all_to_all(blocks, axis, split_axis=0, concat_axis=0, tiled=True)  14.9 us
    ppermute x1, starting transfers between devices, local(): other = lax.ppermute(mine, 'core', SWAP)  11 us
    ppermute x1, starting transfers between devices, local(): taken = lax.ppermute(sent, 'core', SWAP)  5.46 us
  transfers between devices with their start and end apart: 6, of which 5 were waited for; matrix products, arithmetic and copies ran while one was open for 1% of the time, Pallas kernels for 0%

profile of v5, /device:TPU:1, one launch (start us, length us, event | category | flops | bytes accessed | tf_op | source)
XLA Modules:
  0.0 154.9 jit_solution(9623097784654177920)
XLA Ops:
  0.7 1.1 fusion.2
  1.8 16.6 %all_to_all.30 = f32[16,64,128]{2,1,0:T(8,128)S(1)} all-to-all(f32[16,64,128]{2,1,0:T(8,128)S(1)} %broadcast_in_dim.12), channel_id=1, replica_groups=mesh['x'=4,'y'=4,'parity'=8,'pair'=2,'core'=2] {'x','y'}, dimensions={0} | all-to-all | bytes 1048576 | tf_op jit(solution)/shard_map/all_to_all | solution.py:15
  18.5 0.3 convolution_bitcast_fusion
  18.9 9.5 %all_to_all.31 = f32[4,32,128]{2,1,0:T(8,128)S(1)} all-to-all(f32[4,32,128]{2,1,0:T(8,128)S(1)} %bitcast.26), channel_id=1, replica_groups=mesh['x'=4,'y'=4,'parity'=8,'pair'=2,'core'=2] {'pair','core'}, dimensions={0} | all-to-all | bytes 131072 | tf_op jit(solution)/shard_map/all_to_all | solution.py:15
  28.5 0.7 broadcast_in_dim.13
  29.2 14.2 %all-to-all-start.2 = ((f32[8,32,128]{2,1,0:T(8,128)}), f32[8,32,128]{2,1,0:T(8,128)S(1)}, u32[]{:S(2)}, u32[]{:S(2)}) async-start(f32[8,32,128]{2,1,0:T(8,128)} %broadcast_in_dim.13), calls=%async_computation.2 | async-start | bytes 262144 | tf_op jit(solution)/shard_map/all_to_all | solution.py:15
  43.4 1.9 %collective-permute-start = (f32[1024,128]{1,0:T(8,128)S(1)}, f32[1024,128]{1,0:T(8,128)S(1)}, u32[]{:S(2)}, u32[]{:S(2)}) collective-permute-start(f32[1024,128]{1,0:T(8,128)S(1)} %bitcast.24), channel_id=1, source_target_pairs={{0,2},{2,0},{1,3},{3,1},{4,6},{6,4},{5,7},{7,5},{8,10},{10,8},{9,1... | collective-permute-start | bytes 1572872 | tf_op jit(solution)/shard_map/ppermute | solution.py:73
  45.3 11.7 %all-to-all-done.2 = f32[8,32,128]{2,1,0:T(8,128)S(1)} async-done(((f32[8,32,128]{2,1,0:T(8,128)}), f32[8,32,128]{2,1,0:T(8,128)S(1)}, u32[]{:S(2)}, u32[]{:S(2)}) %all-to-all-start.2) | async-done | bytes 131104 | tf_op jit(solution)/shard_map/all_to_all | solution.py:15
  57.0 0.6 broadcast_in_dim.14
  57.6 7.0 %all-to-all-start.3 = ((f32[4,32,128]{2,1,0:T(8,128)}), f32[4,32,128]{2,1,0:T(8,128)S(1)}, u32[]{:S(2)}, u32[]{:S(2)}) async-start(f32[4,32,128]{2,1,0:T(8,128)} %broadcast_in_dim.14), calls=%async_computation.3 | async-start | bytes 131072 | tf_op jit(solution)/shard_map/all_to_all | solution.py:15
  64.6 3.3 %all-to-all-done.3 = f32[4,32,128]{2,1,0:T(8,128)S(1)} async-done(((f32[4,32,128]{2,1,0:T(8,128)}), f32[4,32,128]{2,1,0:T(8,128)S(1)}, u32[]{:S(2)}, u32[]{:S(2)}) %all-to-all-start.3) | async-done | bytes 65568 | tf_op jit(solution)/shard_map/all_to_all | solution.py:15
  67.8 0.2 convolution_bitcast_fusion.1
  68.1 13.2 %all_to_all.32 = f32[16,64,128]{2,1,0:T(8,128)S(1)} all-to-all(f32[16,64,128]{2,1,0:T(8,128)S(1)} %broadcast_in_dim.15), channel_id=1, replica_groups=mesh['x'=4,'y'=4,'parity'=8,'pair'=2,'core'=2] {'x','y'}, dimensions={0} | all-to-all | bytes 1048576 | tf_op jit(solution)/shard_map/all_to_all | solution.py:15
  81.3 1.9 %collective-permute-start.1 = (f32[128,128]{1,0:T(8,128)S(1)}, f32[128,128]{1,0:T(8,128)S(1)}, u32[]{:S(2)}, u32[]{:S(2)}) collective-permute-start(f32[128,128]{1,0:T(8,128)S(1)} %pad_maximum_fusion), channel_id=1, source_target_pairs={{0,2},{2,0},{1,3},{3,1},{4,6},{6,4},{5,7},{7,5},{8,10},{10,8},{9,1... | collective-permute-start | bytes 196616 | tf_op jit(solution)/shard_map/ppermute | solution.py:80
  83.3 0.6 fusion.8
  83.8 2.5 %collective-permute-done.1 = f32[128,128]{1,0:T(8,128)S(1)} collective-permute-done((f32[128,128]{1,0:T(8,128)S(1)}, f32[128,128]{1,0:T(8,128)S(1)}, u32[]{:S(2)}, u32[]{:S(2)}) %collective-permute-start.1) | collective-permute-done | bytes 65568 | tf_op jit(solution)/shard_map/ppermute | solution.py:80
  86.4 0.6 fusion.9
  87.1 5.5 %collective-permute-start.2 = (f32[512,128]{1,0:T(8,128)S(1)}, f32[512,128]{1,0:T(8,128)S(1)}, u32[]{:S(2)}, u32[]{:S(2)}) collective-permute-start(f32[512,128]{1,0:T(8,128)S(1)} %get-tuple-element.40), channel_id=1, source_target_pairs={{0,1},{1,0},{2,3},{3,2},{4,5},{5,4},{6,7},{7,6},{8,9},{9,8},{10,11... | collective-permute-start | bytes 786440 | tf_op jit(solution)/shard_map/ppermute | solution.py:86
  92.6 1.1 collective-permute-done.2
  93.7 23.6 %all_to_all.33 = f32[8,64,128]{2,1,0:T(8,128)S(1)} all-to-all(f32[8,64,128]{2,1,0:T(8,128)S(1)} %bitcast.23), channel_id=1, replica_groups=mesh['x'=4,'y'=4,'parity'=8,'pair'=2,'core'=2] {'parity'}, dimensions={0} | all-to-all | bytes 524288 | tf_op jit(solution)/shard_map/all_to_all | solution.py:15
  117.3 23.9 %all_gather.3 = f32[1024,128]{1,0:T(8,128)S(1)} all-gather(f32[64,128]{1,0:T(8,128)S(1)} %sub.15), channel_id=1, replica_groups=mesh['x'=4,'y'=4,'parity'=8,'pair'=2,'core'=2] {'parity','pair'}, dimensions={0}, use_global_device_ids=true | all-gather | bytes 557056 | tf_op jit(solution)/shard_map/all_gather | solution.py:91
  141.3 11.0 %collective-permute-start.3 = (f32[1024,128]{1,0:T(8,128)S(1)}, f32[1024,128]{1,0:T(8,128)S(1)}, u32[]{:S(2)}, u32[]{:S(2)}) collective-permute-start(f32[1024,128]{1,0:T(8,128)S(1)} %all_gather.3), channel_id=1, source_target_pairs={{0,1},{1,0},{2,3},{3,2},{4,5},{5,4},{6,7},{7,6},{8,9},{9,8},{10,11... | collective-permute-start | bytes 1572872 | tf_op jit(solution)/shard_map/ppermute | solution.py:92
  152.4 1.5 collective-permute-done.3
  153.9 1.1 maximum_select_fusion
  (26 shorter events, 0.6 us)
Async XLA Ops:
  0.6 17.8 %copy-start = (f32[2176,128]{1,0:T(8,128)S(1)}, f32[2176,128]{1,0:T(8,128)}, u32[]{:S(2)}) copy-start(f32[2176,128]{1,0:T(8,128)} %param.4) | copy-start | bytes 3342340
  28.4 39.5 %slice-start = ((f32[2304,128]{1,0:T(8,128)}), f32[128,128]{1,0:T(8,128)S(1)}, s32[]{:S(2)}) async-start(f32[2304,128]{1,0:T(8,128)} %param.3), calls=%async_computation.6 | async-start | bytes 131072 | tf_op jit(solution)/shard_map/slice | solution.py:54
  28.4 39.5 %copy-start.3 = (f32[2,64,128]{2,1,0:T(8,128)S(1)}, f32[2,64,128]{2,1,0:T(8,128)}, u32[]{:S(2)}) copy-start(f32[2,64,128]{2,1,0:T(8,128)} %param.5) | copy-start | bytes 196612
  29.2 27.8 %all-to-all-start.2 = ((f32[8,32,128]{2,1,0:T(8,128)}), f32[8,32,128]{2,1,0:T(8,128)S(1)}, u32[]{:S(2)}, u32[]{:S(2)}) async-start(f32[8,32,128]{2,1,0:T(8,128)} %broadcast_in_dim.13), calls=%async_computation.2 | async-start | bytes 262144 | tf_op jit(solution)/shard_map/all_to_all | solution.py:15
  43.4 21.2 %collective-permute-start = (f32[1024,128]{1,0:T(8,128)S(1)}, f32[1024,128]{1,0:T(8,128)S(1)}, u32[]{:S(2)}, u32[]{:S(2)}) collective-permute-start(f32[1024,128]{1,0:T(8,128)S(1)} %bitcast.24), channel_id=1, source_target_pairs={{0,2},{2,0},{1,3},{3,1},{4,6},{6,4},{5,7},{7,5},{8,10},{10,8},{9,1... | collective-permute-start | bytes 1572872 | tf_op jit(solution)/shard_map/ppermute | solution.py:73
  57.6 10.2 %all-to-all-start.3 = ((f32[4,32,128]{2,1,0:T(8,128)}), f32[4,32,128]{2,1,0:T(8,128)S(1)}, u32[]{:S(2)}, u32[]{:S(2)}) async-start(f32[4,32,128]{2,1,0:T(8,128)} %broadcast_in_dim.14), calls=%async_computation.3 | async-start | bytes 131072 | tf_op jit(solution)/shard_map/all_to_all | solution.py:15
  81.3 5.7 %copy-start.2 = (f32[128,128]{1,0:T(8,128)}, f32[128,128]{1,0:T(8,128)S(1)}, u32[]{:S(2)}) copy-start(f32[128,128]{1,0:T(8,128)S(1)} %pad_maximum_fusion) | copy-start | bytes 196612
  81.3 5.0 %collective-permute-start.1 = (f32[128,128]{1,0:T(8,128)S(1)}, f32[128,128]{1,0:T(8,128)S(1)}, u32[]{:S(2)}, u32[]{:S(2)}) collective-permute-start(f32[128,128]{1,0:T(8,128)S(1)} %pad_maximum_fusion), channel_id=1, source_target_pairs={{0,2},{2,0},{1,3},{3,1},{4,6},{6,4},{5,7},{7,5},{8,10},{10,8},{9,1... | collective-permute-start | bytes 196616 | tf_op jit(solution)/shard_map/ppermute | solution.py:80
  86.9 5.6 %copy-start.1 = (f32[2304,128]{1,0:T(8,128)S(1)}, f32[2304,128]{1,0:T(8,128)}, u32[]{:S(2)}) copy-start(f32[2304,128]{1,0:T(8,128)} %param.3) | copy-start | bytes 3538948
  87.1 6.6 %collective-permute-start.2 = (f32[512,128]{1,0:T(8,128)S(1)}, f32[512,128]{1,0:T(8,128)S(1)}, u32[]{:S(2)}, u32[]{:S(2)}) collective-permute-start(f32[512,128]{1,0:T(8,128)S(1)} %get-tuple-element.40), channel_id=1, source_target_pairs={{0,1},{1,0},{2,3},{3,2},{4,5},{5,4},{6,7},{7,6},{8,9},{9,8},{10,11... | collective-permute-start | bytes 786440 | tf_op jit(solution)/shard_map/ppermute | solution.py:86
  141.3 12.6 %collective-permute-start.3 = (f32[1024,128]{1,0:T(8,128)S(1)}, f32[1024,128]{1,0:T(8,128)S(1)}, u32[]{:S(2)}, u32[]{:S(2)}) collective-permute-start(f32[1024,128]{1,0:T(8,128)S(1)} %all_gather.3), channel_id=1, source_target_pairs={{0,1},{1,0},{2,3},{3,2},{4,5},{5,4},{6,7},{7,6},{8,9},{9,8},{10,11... | collective-permute-start | bytes 1572872 | tf_op jit(solution)/shard_map/ppermute | solution.py:92

commit v6 on v4

--- a/solution.py
+++ b/solution.py
@@ -1,6 +1,7 @@
 import jax
 import jax.numpy as jnp
 from jax import lax
+from jax.experimental.layout import Layout, with_layout_constraint
 from jax.sharding import Mesh
 from jax.sharding import PartitionSpec as P
 
@@ -29,16 +30,12 @@
     return jnp.sum(exchanged(blocks, axis), axis=0)
 
 
-def gathered(array, axis):
-    return from_everyone(array, axis).reshape(-1, *array.shape[1:])
-
-
 def product(left, right):
     return jnp.dot(left, right, precision=lax.Precision.HIGHEST, preferred_element_type=jnp.float32)
 
 
 def part_of(array, start, rows):
-    return lax.dynamic_slice(array, (start, jnp.uint32(0)), (rows, array.shape[1]))
+    return lax.dynamic_slice(array, (start, 0), (rows, array.shape[1]), allow_negative_indices=False)
 
 
 def local(rhs, factor, inverses):
@@ -49,22 +46,30 @@
     spots = lax.axis_size(Z)
     rows = (rhs.shape[0] - 2 * span_rows) // (2 * spots)
     half = spots * rows
-    core = lax.axis_index("core").astype(jnp.uint32)
-    pair = lax.axis_index("pair").astype(jnp.uint32)
+    core = lax.axis_index("core")
+    pair = lax.axis_index("pair")
     quarter = half // 2
-    place = 2 * span_rows + core * half + lax.axis_index(Z).astype(jnp.uint32) * rows
-    starts = (core * half, (1 - core) * half, pair * quarter, (1 - pair) * quarter, place)
+    place = 2 * span_rows + core * half + lax.axis_index(Z) * rows
+    near_rows = span_rows // lax.axis_size(NEAR)
+    near = lax.axis_index(NEAR) * near_rows
+    starts = (core * half, (1 - core) * half, pair * quarter, (1 - pair) * quarter, near, place)
     first_part = product(inverses[0], first_rhs)
     first_part, second_rhs, starts = lax.optimization_barrier((first_part, second_rhs, starts))
-    half_kept, half_sent, quarter_kept, quarter_sent, place = starts
+    half_kept, half_sent, quarter_kept, quarter_sent, near, place = starts
 
     first_sol = taken_together(first_part, ROW)
     coupled = lax.optimization_barrier(product(factor[:span_rows, :span_cols], first_sol))
-    coupled = gathered(taken_together(my_sum(coupled, NEAR), "parity"), NEAR)
+    coupled = with_layout_constraint(coupled, Layout((0, 1)))
+    coupled = lax.all_gather(coupled, NEAR, axis=0)
+    coupled = lax.dynamic_slice(
+        coupled, (0, near, 0), (coupled.shape[0], near_rows, coupled.shape[2]), allow_negative_indices=False
+    )
+    coupled = taken_together(jnp.sum(coupled, axis=0), "parity")
+    coupled = lax.all_gather(coupled, NEAR, axis=0, tiled=True)
     second_sol = taken_together(product(inverses[1], second_rhs - coupled), ROW)
 
     both = lax.optimization_barrier(jnp.concatenate([first_sol, second_sol], 0))
-    terms = product(factor[span_rows:], both)
+    terms = with_layout_constraint(product(factor[span_rows:], both), Layout((0, 1)))
     terms = terms.reshape(2, spots // 2, 2, rows, -1).swapaxes(1, 2).reshape(2 * half, -1)
     sent, kept = part_of(terms, half_sent, half), part_of(terms, half_kept, half)
     sent, kept, rhs = lax.optimization_barrier((sent, kept, rhs))
@@ -73,7 +78,8 @@
     taken, trailing = lax.optimization_barrier((taken, trailing))
     terms = kept + taken
     sent, kept = part_of(terms, quarter_sent, quarter), part_of(terms, quarter_kept, quarter)
-    terms = my_sum(kept + lax.ppermute(sent, "pair", SWAP), "parity")
+    taken = part_of(lax.all_gather(sent, "pair", axis=0, tiled=True), quarter_sent, quarter)
+    terms = my_sum(kept + taken, "parity")
 
     mine = lax.all_gather(trailing - terms, Z, axis=0, tiled=True)
     other = lax.ppermute(mine, "core", SWAP)

time: 153 us -> 152 us (level)
  blocking collectives: 120 us -> 129 us
  waiting for transfers between devices: 10.5 us -> 2.99 us
    all_gather x0 -> x3, blocking collectives: none -> 25.9 us  [the longest x1 9.24 us: local(): coupled = lax.all_gather(coupled, NEAR, axis=0)]
    all_to_all x6 -> x4, blocking collectives: 94.8 us -> 76.8 us  [exchanged(): return lax.all_to_all(blocks, axis, split_axis=0, concat_axis=0, tiled=True)]
    ppermute x1 -> x0, waiting for transfers between devices: 7.49 us -> none  [local(): terms = my_sum(kept + lax.ppermute(sent, 'pair', SWAP), 'parity')]
    ppermute x1 -> x0, starting transfers between devices: 1.92 us -> none  [local(): terms = my_sum(kept + lax.ppermute(sent, 'pair', SWAP), 'parity')]
  transfers between devices with their start and end apart: 3 -> 2, of which waited for: 3 -> 2; matrix products, arithmetic and copies ran while one was open for 0% -> 0% of each run, Pallas kernels for 0% -> 0%
where the time goes in v6:
time: 152 us; the launch traced here: 151 us
  blocking collectives  129 us (85%)
  starting transfers between devices  14.8 us (10%)
  waiting for transfers between devices  2.99 us (2%)
  matrix products  2.39 us (2%)
    all_to_all x4, blocking collectives, exchanged(): return lax.all_to_all(blocks, axis, split_axis=0, concat_axis=0, tiled=True)  76.8 us
    all_gather x1, blocking collectives, local(): mine = lax.all_gather(trailing - terms, Z, axis=0, tiled=True)  26.1 us
    ppermute x1, starting transfers between devices, local(): other = lax.ppermute(mine, 'core', SWAP)  10.5 us
    all_gather x1, blocking collectives, local(): coupled = lax.all_gather(coupled, NEAR, axis=0)  9.24 us
    all_gather x1, blocking collectives, local(): coupled = lax.all_gather(coupled, NEAR, axis=0, tiled=True)  8.44 us
    all_gather x1, blocking collectives, local(): lax.all_gather(sent, 'pair', axis=0, tiled=True)  8.2 us
    ppermute x1, starting transfers between devices, local(): taken = lax.ppermute(sent, 'core', SWAP)  4.3 us
  transfers between devices with their start and end apart: 2, of which 2 were waited for; matrix products, arithmetic and copies ran while one was open for 0% of the time, Pallas kernels for 0%

profile of v6, /device:TPU:1, one launch (start us, length us, event | category | flops | bytes accessed | tf_op | source)
XLA Modules:
  0.0 151.5 jit_solution(5168134846005453875)
XLA Ops:
  0.6 1.0 fusion.4
  1.7 0.0 copy-start
  1.8 16.7 %all_to_all.20 = f32[16,64,128]{2,1,0:T(8,128)S(1)} all-to-all(f32[16,64,128]{2,1,0:T(8,128)S(1)} %broadcast_in_dim.9), channel_id=1, replica_groups=mesh['x'=4,'y'=4,'parity'=8,'pair'=2,'core'=2] {'x','y'}, dimensions={0} | all-to-all | bytes 1048576 | tf_op jit(solution)/shard_map/all_to_all | solution.py:16
  18.5 0.2 convolution_bitcast_fusion
  18.8 9.2 %all-gather = f32[512,128]{1,0:T(8,128)S(1)} all-gather(f32[128,128]{1,0:T(8,128)S(1)} %convolution_bitcast_fusion), channel_id=2, replica_groups=mesh['x'=4,'y'=4,'parity'=8,'pair'=2,'core'=2] {'pair','core'}, dimensions={0}, use_global_device_ids=true | all-gather | bytes 327680 | tf_op jit(solution)/shard_map/all_gather | solution.py:63
  28.0 27.8 %all_to_all.21 = f32[8,32,128]{2,1,0:T(8,128)S(1)} all-to-all(f32[8,32,128]{2,1,0:T(8,128)S(1)} %broadcast_in_dim.10), channel_id=1, replica_groups=mesh['x'=4,'y'=4,'parity'=8,'pair'=2,'core'=2] {'parity'}, dimensions={0} | all-to-all | bytes 262144 | tf_op jit(solution)/shard_map/all_to_all | solution.py:16
  55.8 8.4 %all_gather.17 = f32[128,128]{1,0:T(8,128)S(1)} all-gather(f32[32,128]{1,0:T(8,128)S(1)} %reduce_sum.47), channel_id=1, replica_groups=mesh['x'=4,'y'=4,'parity'=8,'pair'=2,'core'=2] {'pair','core'}, dimensions={0}, use_global_device_ids=true | all-gather | bytes 81920 | tf_op jit(solution)/shard_map/all_gather | solution.py:68
  64.3 0.2 convolution_bitcast_fusion.1
  64.5 13.2 %all_to_all.22 = f32[16,64,128]{2,1,0:T(8,128)S(1)} all-to-all(f32[16,64,128]{2,1,0:T(8,128)S(1)} %broadcast_in_dim.11), channel_id=1, replica_groups=mesh['x'=4,'y'=4,'parity'=8,'pair'=2,'core'=2] {'x','y'}, dimensions={0} | all-to-all | bytes 1048576 | tf_op jit(solution)/shard_map/all_to_all | solution.py:16
  77.8 0.0 copy-start.1
  77.8 1.0 fusion
  78.8 0.1 copy.9
  78.9 0.0 copy-start.2
  78.9 0.1 constant_dynamic-slice_fusion.2
  79.0 4.3 %collective-permute-start = (f32[1024,128]{1,0:T(8,128)S(1)}, f32[1024,128]{1,0:T(8,128)S(1)}, u32[]{:S(2)}, u32[]{:S(2)}) collective-permute-start(f32[1024,128]{1,0:T(8,128)S(1)} %get-tuple-element.20), channel_id=1, source_target_pairs={{0,1},{1,0},{2,3},{3,2},{4,5},{5,4},{6,7},{7,6},{8,9},{9,8},{10,11... | collective-permute-start | bytes 1572872 | tf_op jit(solution)/shard_map/ppermute | solution.py:76
  83.3 1.5 collective-permute-done
  84.8 0.1 add.18
  84.9 8.2 %all_gather.18 = f32[1024,128]{1,0:T(8,128)S(1)} all-gather(f32[512,128]{1,0:T(8,128)S(1)} %constant_dynamic-slice_fusion), channel_id=1, replica_groups=mesh['x'=4,'y'=4,'parity'=8,'pair'=2,'core'=2] {'pair'}, dimensions={0}, use_global_device_ids=true | all-gather | bytes 786432 | tf_op jit(solution)/shard_map/all_gather | solution.py:81
  93.1 0.1 dynamic-slice_add_fusion
  93.2 19.1 %all_to_all.23 = f32[8,64,128]{2,1,0:T(8,128)S(1)} all-to-all(f32[8,64,128]{2,1,0:T(8,128)S(1)} %bitcast.22), channel_id=1, replica_groups=mesh['x'=4,'y'=4,'parity'=8,'pair'=2,'core'=2] {'parity'}, dimensions={0} | all-to-all | bytes 524288 | tf_op jit(solution)/shard_map/all_to_all | solution.py:16
  112.3 26.1 %all_gather.19 = f32[1024,128]{1,0:T(8,128)S(1)} all-gather(f32[64,128]{1,0:T(8,128)S(1)} %sub.15), channel_id=1, replica_groups=mesh['x'=4,'y'=4,'parity'=8,'pair'=2,'core'=2] {'parity','pair'}, dimensions={0}, use_global_device_ids=true | all-gather | bytes 557056 | tf_op jit(solution)/shard_map/all_gather | solution.py:84
  138.4 10.5 %collective-permute-start.1 = (f32[1024,128]{1,0:T(8,128)S(1)}, f32[1024,128]{1,0:T(8,128)S(1)}, u32[]{:S(2)}, u32[]{:S(2)}) collective-permute-start(f32[1024,128]{1,0:T(8,128)S(1)} %all_gather.19), channel_id=1, source_target_pairs={{0,1},{1,0},{2,3},{3,2},{4,5},{5,4},{6,7},{7,6},{8,9},{9,8},{10,11... | collective-permute-start | bytes 1572872 | tf_op jit(solution)/shard_map/ppermute | solution.py:85
  148.9 1.5 collective-permute-done.1
  150.4 1.1 maximum_select_fusion
  (19 shorter events, 0.3 us)
Async XLA Ops:
  1.7 16.8 %copy-start = (f32[2176,128]{1,0:T(8,128)S(1)}, f32[2176,128]{1,0:T(8,128)}, u32[]{:S(2)}) copy-start(f32[2176,128]{1,0:T(8,128)} %param.4) | copy-start | bytes 3342340
  18.5 45.8 %slice-start = ((f32[2304,128]{1,0:T(8,128)}), f32[128,128]{1,0:T(8,128)S(1)}, s32[]{:S(2)}) async-start(f32[2304,128]{1,0:T(8,128)} %param.3), calls=%async_computation.4 | async-start | bytes 131072 | tf_op jit(solution)/shard_map/slice | solution.py:45
  18.5 45.8 %copy-start.3 = (f32[2,64,128]{2,1,0:T(8,128)S(1)}, f32[2,64,128]{2,1,0:T(8,128)}, u32[]{:S(2)}) copy-start(f32[2,64,128]{2,1,0:T(8,128)} %param.5) | copy-start | bytes 196612
  77.8 1.1 copy-start.1
  78.9 4.4 %copy-start.2 = (f32[2304,128]{1,0:T(8,128)S(1)}, f32[2304,128]{1,0:T(8,128)}, u32[]{:S(2)}) copy-start(f32[2304,128]{1,0:T(8,128)} %param.3) | copy-start | bytes 3538948
  79.0 5.8 %collective-permute-start = (f32[1024,128]{1,0:T(8,128)S(1)}, f32[1024,128]{1,0:T(8,128)S(1)}, u32[]{:S(2)}, u32[]{:S(2)}) collective-permute-start(f32[1024,128]{1,0:T(8,128)S(1)} %get-tuple-element.20), channel_id=1, source_target_pairs={{0,1},{1,0},{2,3},{3,2},{4,5},{5,4},{6,7},{7,6},{8,9},{9,8},{10,11... | collective-permute-start | bytes 1572872 | tf_op jit(solution)/shard_map/ppermute | solution.py:76
  138.4 12.0 %collective-permute-start.1 = (f32[1024,128]{1,0:T(8,128)S(1)}, f32[1024,128]{1,0:T(8,128)S(1)}, u32[]{:S(2)}, u32[]{:S(2)}) collective-permute-start(f32[1024,128]{1,0:T(8,128)S(1)} %all_gather.19), channel_id=1, source_target_pairs={{0,1},{1,0},{2,3},{3,2},{4,5},{5,4},{6,7},{7,6},{8,9},{9,8},{10,11... | collective-permute-start | bytes 1572872 | tf_op jit(solution)/shard_map/ppermute | solution.py:85

commit v7 on v6

--- a/solution.py
+++ b/solution.py
@@ -10,6 +10,7 @@
 Z = ("parity", "pair")
 COL = (*Z, "core")
 SWAP = [(0, 1), (1, 0)]
+CROSSED = [[0, 3], [1, 2]]
 
 
 def exchanged(blocks, axis):
@@ -46,13 +47,13 @@
     spots = lax.axis_size(Z)
     rows = (rhs.shape[0] - 2 * span_rows) // (2 * spots)
     half = spots * rows
-    core = lax.axis_index("core")
+    side = lax.axis_index("core") ^ lax.axis_index("pair")
     pair = lax.axis_index("pair")
     quarter = half // 2
-    place = 2 * span_rows + core * half + lax.axis_index(Z) * rows
+    place = 2 * span_rows + side * half + lax.axis_index(Z) * rows
     near_rows = span_rows // lax.axis_size(NEAR)
     near = lax.axis_index(NEAR) * near_rows
-    starts = (core * half, (1 - core) * half, pair * quarter, (1 - pair) * quarter, near, place)
+    starts = (side * half, (1 - side) * half, pair * quarter, (1 - pair) * quarter, near, place)
     first_part = product(inverses[0], first_rhs)
     first_part, second_rhs, starts = lax.optimization_barrier((first_part, second_rhs, starts))
     half_kept, half_sent, quarter_kept, quarter_sent, near, place = starts
@@ -78,13 +79,15 @@
     taken, trailing = lax.optimization_barrier((taken, trailing))
     terms = kept + taken
     sent, kept = part_of(terms, quarter_sent, quarter), part_of(terms, quarter_kept, quarter)
-    taken = part_of(lax.all_gather(sent, "pair", axis=0, tiled=True), quarter_sent, quarter)
+    sent = lax.all_gather(sent, NEAR, axis=0, tiled=True, axis_index_groups=CROSSED)
+    taken = part_of(sent, quarter_sent, quarter)
     terms = my_sum(kept + taken, "parity")
 
-    mine = lax.all_gather(trailing - terms, Z, axis=0, tiled=True)
+    rings = [[2 * z + (z + start) % 2 for z in range(spots)] for start in range(2)]
+    mine = lax.all_gather(trailing - terms, COL, axis=0, tiled=True, axis_index_groups=rings)
     other = lax.ppermute(mine, "core", SWAP)
     remaining = jnp.where(
-        lax.axis_index("core") == 0, jnp.concatenate([mine, other], 0), jnp.concatenate([other, mine], 0)
+        side == 0, jnp.concatenate([mine, other], 0), jnp.concatenate([other, mine], 0)
     )
     return (both, remaining)
 

time: 152 us -> 149 us (0.980)
  starting transfers between devices: 14.8 us -> 6.71 us
  blocking collectives: 129 us -> 134 us
    ppermute x1, starting transfers between devices: 10.5 us -> 2.42 us  [local(): other = lax.ppermute(mine, 'core', SWAP)]
    all_to_all x4, blocking collectives: 76.8 us -> 81.6 us  [exchanged(): return lax.all_to_all(blocks, axis, split_axis=0, concat_axis=0, tiled=True)]
where the time goes in v7:
time: 149 us; the launch traced here: 148 us
  blocking collectives  134 us (90%)
  starting transfers between devices  6.71 us (5%)
  waiting for transfers between devices  2.99 us (2%)
  matrix products  2.4 us (2%)
    all_to_all x4, blocking collectives, exchanged(): return lax.all_to_all(blocks, axis, split_axis=0, concat_axis=0, tiled=True)  81.6 us
    all_gather x1, blocking collectives, local(): lax.all_gather(trailing - terms, COL, axis=0, tiled=True, axis_index_grou...  25.6 us
    all_gather x1, blocking collectives, local(): coupled = lax.all_gather(coupled, NEAR, axis=0)  9.24 us
    all_gather x1, blocking collectives, local(): lax.all_gather(sent, NEAR, axis=0, tiled=True, axis_index_groups=CROSSED)  8.97 us
    all_gather x1, blocking collectives, local(): coupled = lax.all_gather(coupled, NEAR, axis=0, tiled=True)  8.44 us
    ppermute x1, starting transfers between devices, local(): taken = lax.ppermute(sent, 'core', SWAP)  4.29 us
  transfers between devices with their start and end apart: 2, of which 2 were waited for; matrix products, arithmetic and copies ran while one was open for 0% of the time, Pallas kernels for 0%

profile of v7, /device:TPU:1, one launch (start us, length us, event | category | flops | bytes accessed | tf_op | source)
XLA Modules:
  0.0 148.5 jit_solution(9372318556893751723)
XLA Ops:
  0.6 1.0 fusion.4
  1.7 0.0 copy-start
  1.8 16.7 %all_to_all.20 = f32[16,64,128]{2,1,0:T(8,128)S(1)} all-to-all(f32[16,64,128]{2,1,0:T(8,128)S(1)} %broadcast_in_dim.9), channel_id=1, replica_groups=mesh['x'=4,'y'=4,'parity'=8,'pair'=2,'core'=2] {'x','y'}, dimensions={0} | all-to-all | bytes 1048576 | tf_op jit(solution)/shard_map/all_to_all | solution.py:17
  18.5 0.2 convolution_bitcast_fusion
  18.8 9.2 %all-gather = f32[512,128]{1,0:T(8,128)S(1)} all-gather(f32[128,128]{1,0:T(8,128)S(1)} %convolution_bitcast_fusion), channel_id=2, replica_groups=mesh['x'=4,'y'=4,'parity'=8,'pair'=2,'core'=2] {'pair','core'}, dimensions={0}, use_global_device_ids=true | all-gather | bytes 327680 | tf_op jit(solution)/shard_map/all_gather | solution.py:64
  28.0 27.8 %all_to_all.21 = f32[8,32,128]{2,1,0:T(8,128)S(1)} all-to-all(f32[8,32,128]{2,1,0:T(8,128)S(1)} %broadcast_in_dim.10), channel_id=1, replica_groups=mesh['x'=4,'y'=4,'parity'=8,'pair'=2,'core'=2] {'parity'}, dimensions={0} | all-to-all | bytes 262144 | tf_op jit(solution)/shard_map/all_to_all | solution.py:17
  55.8 8.4 %all_gather.17 = f32[128,128]{1,0:T(8,128)S(1)} all-gather(f32[32,128]{1,0:T(8,128)S(1)} %reduce_sum.47), channel_id=1, replica_groups=mesh['x'=4,'y'=4,'parity'=8,'pair'=2,'core'=2] {'pair','core'}, dimensions={0}, use_global_device_ids=true | all-gather | bytes 81920 | tf_op jit(solution)/shard_map/all_gather | solution.py:69
  64.3 0.2 convolution_bitcast_fusion.1
  64.5 13.2 %all_to_all.22 = f32[16,64,128]{2,1,0:T(8,128)S(1)} all-to-all(f32[16,64,128]{2,1,0:T(8,128)S(1)} %broadcast_in_dim.11), channel_id=1, replica_groups=mesh['x'=4,'y'=4,'parity'=8,'pair'=2,'core'=2] {'x','y'}, dimensions={0} | all-to-all | bytes 1048576 | tf_op jit(solution)/shard_map/all_to_all | solution.py:17
  77.8 0.0 copy-start.1
  77.8 1.0 fusion
  78.8 0.1 copy.9
  78.9 0.0 copy-start.2
  78.9 0.1 constant_dynamic-slice_fusion.2
  79.0 4.3 %collective-permute-start = (f32[1024,128]{1,0:T(8,128)S(1)}, f32[1024,128]{1,0:T(8,128)S(1)}, u32[]{:S(2)}, u32[]{:S(2)}) collective-permute-start(f32[1024,128]{1,0:T(8,128)S(1)} %get-tuple-element.20), channel_id=1, source_target_pairs={{0,1},{1,0},{2,3},{3,2},{4,5},{5,4},{6,7},{7,6},{8,9},{9,8},{10,11... | collective-permute-start | bytes 1572872 | tf_op jit(solution)/shard_map/ppermute | solution.py:77
  83.3 1.5 collective-permute-done
  84.8 0.1 add.18
  84.9 9.0 %all_gather.18 = f32[1024,128]{1,0:T(8,128)S(1)} all-gather(f32[512,128]{1,0:T(8,128)S(1)} %constant_dynamic-slice_fusion), channel_id=1, replica_groups={{0,3},{1,2},{4,7},{5,6},{8,11},{9,10},{12,15},{13,14},{16,19},{17,18},{..., dimensions={0}, use_global_device_ids=true | all-gather | bytes 786432 | tf_op jit(solution)/shard_map/all_gather | solution.py:82
  93.9 0.1 dynamic-slice_add_fusion
  94.0 23.9 %all_to_all.23 = f32[8,64,128]{2,1,0:T(8,128)S(1)} all-to-all(f32[8,64,128]{2,1,0:T(8,128)S(1)} %bitcast.22), channel_id=1, replica_groups=mesh['x'=4,'y'=4,'parity'=8,'pair'=2,'core'=2] {'parity'}, dimensions={0} | all-to-all | bytes 524288 | tf_op jit(solution)/shard_map/all_to_all | solution.py:17
  117.9 25.6 %all_gather.19 = f32[1024,128]{1,0:T(8,128)S(1)} all-gather(f32[64,128]{1,0:T(8,128)S(1)} %sub.15), channel_id=1, replica_groups={{0,3,4,7,8,11,12,15,16,19,20,23,24,27,28,31},{1,2,5,6,9,10,13,14,17,18,..., dimensions={0}, use_global_device_ids=true | all-gather | bytes 557056 | tf_op jit(solution)/shard_map/all_gather | solution.py:87
  143.4 2.4 %collective-permute-start.1 = (f32[1024,128]{1,0:T(8,128)S(1)}, f32[1024,128]{1,0:T(8,128)S(1)}, u32[]{:S(2)}, u32[]{:S(2)}) collective-permute-start(f32[1024,128]{1,0:T(8,128)S(1)} %all_gather.19), channel_id=1, source_target_pairs={{0,1},{1,0},{2,3},{3,2},{4,5},{5,4},{6,7},{7,6},{8,9},{9,8},{10,11... | collective-permute-start | bytes 1572872 | tf_op jit(solution)/shard_map/ppermute | solution.py:88
  145.9 1.5 %collective-permute-done.1 = f32[1024,128]{1,0:T(8,128)S(1)} collective-permute-done((f32[1024,128]{1,0:T(8,128)S(1)}, f32[1024,128]{1,0:T(8,128)S(1)}, u32[]{:S(2)}, u32[]{:S(2)}) %collective-permute-start.1) | collective-permute-done | bytes 524320 | tf_op jit(solution)/shard_map/ppermute | solution.py:88
  147.4 1.1 maximum_select_fusion
  (19 shorter events, 0.3 us)
Async XLA Ops:
  1.7 16.8 %copy-start = (f32[2176,128]{1,0:T(8,128)S(1)}, f32[2176,128]{1,0:T(8,128)}, u32[]{:S(2)}) copy-start(f32[2176,128]{1,0:T(8,128)} %param.4) | copy-start | bytes 3342340
  18.5 45.8 %slice-start = ((f32[2304,128]{1,0:T(8,128)}), f32[128,128]{1,0:T(8,128)S(1)}, s32[]{:S(2)}) async-start(f32[2304,128]{1,0:T(8,128)} %param.3), calls=%async_computation.4 | async-start | bytes 131072 | tf_op jit(solution)/shard_map/slice | solution.py:46
  18.5 45.8 %copy-start.3 = (f32[2,64,128]{2,1,0:T(8,128)S(1)}, f32[2,64,128]{2,1,0:T(8,128)}, u32[]{:S(2)}) copy-start(f32[2,64,128]{2,1,0:T(8,128)} %param.5) | copy-start | bytes 196612
  77.8 1.1 copy-start.1
  78.9 4.4 %copy-start.2 = (f32[2304,128]{1,0:T(8,128)S(1)}, f32[2304,128]{1,0:T(8,128)}, u32[]{:S(2)}) copy-start(f32[2304,128]{1,0:T(8,128)} %param.3) | copy-start | bytes 3538948
  79.0 5.8 %collective-permute-start = (f32[1024,128]{1,0:T(8,128)S(1)}, f32[1024,128]{1,0:T(8,128)S(1)}, u32[]{:S(2)}, u32[]{:S(2)}) collective-permute-start(f32[1024,128]{1,0:T(8,128)S(1)} %get-tuple-element.20), channel_id=1, source_target_pairs={{0,1},{1,0},{2,3},{3,2},{4,5},{5,4},{6,7},{7,6},{8,9},{9,8},{10,11... | collective-permute-start | bytes 1572872 | tf_op jit(solution)/shard_map/ppermute | solution.py:77
  143.4 3.9 %collective-permute-start.1 = (f32[1024,128]{1,0:T(8,128)S(1)}, f32[1024,128]{1,0:T(8,128)S(1)}, u32[]{:S(2)}, u32[]{:S(2)}) collective-permute-start(f32[1024,128]{1,0:T(8,128)S(1)} %all_gather.19), channel_id=1, source_target_pairs={{0,1},{1,0},{2,3},{3,2},{4,5},{5,4},{6,7},{7,6},{8,9},{9,8},{10,11... | collective-permute-start | bytes 1572872 | tf_op jit(solution)/shard_map/ppermute | solution.py:88

commit v8 on v7

--- a/solution.py
+++ b/solution.py
@@ -31,8 +31,8 @@
     return jnp.sum(exchanged(blocks, axis), axis=0)
 
 
-def product(left, right):
-    return jnp.dot(left, right, precision=lax.Precision.HIGHEST, preferred_element_type=jnp.float32)
+def product(left, right, precision=lax.Precision.HIGHEST):
+    return jnp.dot(left, right, precision=precision, preferred_element_type=jnp.float32)
 
 
 def part_of(array, start, rows):
@@ -51,8 +51,8 @@
     pair = lax.axis_index("pair")
     quarter = half // 2
     place = 2 * span_rows + side * half + lax.axis_index(Z) * rows
-    near_rows = span_rows // lax.axis_size(NEAR)
-    near = lax.axis_index(NEAR) * near_rows
+    near_rows = span_rows // 2
+    near = lax.axis_index("core") * near_rows
     starts = (side * half, (1 - side) * half, pair * quarter, (1 - pair) * quarter, near, place)
     first_part = product(inverses[0], first_rhs)
     first_part, second_rhs, starts = lax.optimization_barrier((first_part, second_rhs, starts))
@@ -66,11 +66,11 @@
         coupled, (0, near, 0), (coupled.shape[0], near_rows, coupled.shape[2]), allow_negative_indices=False
     )
     coupled = taken_together(jnp.sum(coupled, axis=0), "parity")
-    coupled = lax.all_gather(coupled, NEAR, axis=0, tiled=True)
+    coupled = lax.all_gather(coupled, "core", axis=0, tiled=True)
     second_sol = taken_together(product(inverses[1], second_rhs - coupled), ROW)
 
     both = lax.optimization_barrier(jnp.concatenate([first_sol, second_sol], 0))
-    terms = with_layout_constraint(product(factor[span_rows:], both), Layout((0, 1)))
+    terms = with_layout_constraint(product(factor[span_rows:], both, lax.Precision.HIGH), Layout((0, 1)))
     terms = terms.reshape(2, spots // 2, 2, rows, -1).swapaxes(1, 2).reshape(2 * half, -1)
     sent, kept = part_of(terms, half_sent, half), part_of(terms, half_kept, half)
     sent, kept, rhs = lax.optimization_barrier((sent, kept, rhs))

time: 149 us -> 150 us (level)
  blocking collectives: 134 us -> 136 us
    all_to_all x4, blocking collectives: 81.6 us -> 88.1 us  [exchanged(): return lax.all_to_all(blocks, axis, split_axis=0, concat_axis=0, tiled=True)]
    all_gather x1, blocking collectives: 8.44 us -> 2.03 us  [local(): coupled = lax.all_gather(coupled, 'core', axis=0, tiled=True)]
    all_gather x1, blocking collectives: 25.6 us -> 27.6 us  [local(): lax.all_gather(trailing - terms, COL, axis=0, tiled=True, axis_index_grou...]
where the time goes in v8:
time: 150 us
  blocking collectives  136 us (91%)
  starting transfers between devices  6.25 us (4%)
  waiting for transfers between devices  3.13 us (2%)
  matrix products  1.99 us (1%)
    all_to_all x4, blocking collectives, exchanged(): return lax.all_to_all(blocks, axis, split_axis=0, concat_axis=0, tiled=True)  88.1 us
    all_gather x1, blocking collectives, local(): lax.all_gather(trailing - terms, COL, axis=0, tiled=True, axis_index_grou...  27.6 us
    all_gather x1, blocking collectives, local(): coupled = lax.all_gather(coupled, NEAR, axis=0)  9.24 us
    all_gather x1, blocking collectives, local(): lax.all_gather(sent, NEAR, axis=0, tiled=True, axis_index_groups=CROSSED)  8.97 us
    ppermute x1, starting transfers between devices, local(): taken = lax.ppermute(sent, 'core', SWAP)  4.11 us
  transfers between devices with their start and end apart: 2, of which 2 were waited for; matrix products, arithmetic and copies ran while one was open for 0% of the time, Pallas kernels for 0%

profile of v8, /device:TPU:1, one launch (start us, length us, event | category | flops | bytes accessed | tf_op | source)
XLA Modules:
  0.0 149.9 jit_solution(1970071990622430372)
XLA Ops:
  0.6 1.0 fusion.4
  1.7 0.0 copy-start
  1.8 16.7 %all_to_all.20 = f32[16,64,128]{2,1,0:T(8,128)S(1)} all-to-all(f32[16,64,128]{2,1,0:T(8,128)S(1)} %broadcast_in_dim.9), channel_id=1, replica_groups=mesh['x'=4,'y'=4,'parity'=8,'pair'=2,'core'=2] {'x','y'}, dimensions={0} | all-to-all | bytes 1048576 | tf_op jit(solution)/shard_map/all_to_all | solution.py:17
  18.5 0.2 convolution_bitcast_fusion
  18.7 9.2 %all-gather = f32[512,128]{1,0:T(8,128)S(1)} all-gather(f32[128,128]{1,0:T(8,128)S(1)} %convolution_bitcast_fusion), channel_id=2, replica_groups=mesh['x'=4,'y'=4,'parity'=8,'pair'=2,'core'=2] {'pair','core'}, dimensions={0}, use_global_device_ids=true | all-gather | bytes 327680 | tf_op jit(solution)/shard_map/all_gather | solution.py:64
  28.0 36.0 %all_to_all.21 = f32[8,64,128]{2,1,0:T(8,128)S(1)} all-to-all(f32[8,64,128]{2,1,0:T(8,128)S(1)} %broadcast_in_dim.10), channel_id=1, replica_groups=mesh['x'=4,'y'=4,'parity'=8,'pair'=2,'core'=2] {'parity'}, dimensions={0} | all-to-all | bytes 524288 | tf_op jit(solution)/shard_map/all_to_all | solution.py:17
  64.1 2.0 %all_gather.17 = f32[128,128]{1,0:T(8,128)S(1)} all-gather(f32[64,128]{1,0:T(8,128)S(1)} %reduce_sum.47), channel_id=1, replica_groups=mesh['x'=4,'y'=4,'parity'=8,'pair'=2,'core'=2] {'core'}, dimensions={0}, use_global_device_ids=true | all-gather | bytes 98304 | tf_op jit(solution)/shard_map/all_gather | solution.py:69
  66.1 0.2 convolution_bitcast_fusion.1
  66.4 13.4 %all_to_all.22 = f32[16,64,128]{2,1,0:T(8,128)S(1)} all-to-all(f32[16,64,128]{2,1,0:T(8,128)S(1)} %broadcast_in_dim.11), channel_id=1, replica_groups=mesh['x'=4,'y'=4,'parity'=8,'pair'=2,'core'=2] {'x','y'}, dimensions={0} | all-to-all | bytes 1048576 | tf_op jit(solution)/shard_map/all_to_all | solution.py:17
  79.8 0.0 copy-start.1
  79.8 0.6 fusion
  80.4 0.1 copy.9
  80.5 0.0 copy-start.2
  80.5 0.1 constant_dynamic-slice_fusion.2
  80.6 4.1 %collective-permute-start = (f32[1024,128]{1,0:T(8,128)S(1)}, f32[1024,128]{1,0:T(8,128)S(1)}, u32[]{:S(2)}, u32[]{:S(2)}) collective-permute-start(f32[1024,128]{1,0:T(8,128)S(1)} %get-tuple-element.20), channel_id=1, source_target_pairs={{0,1},{1,0},{2,3},{3,2},{4,5},{5,4},{6,7},{7,6},{8,9},{9,8},{10,11... | collective-permute-start | bytes 1572872 | tf_op jit(solution)/shard_map/ppermute | solution.py:77
  84.8 1.5 collective-permute-done
  86.2 0.1 add.14
  86.4 9.0 %all_gather.18 = f32[1024,128]{1,0:T(8,128)S(1)} all-gather(f32[512,128]{1,0:T(8,128)S(1)} %constant_dynamic-slice_fusion), channel_id=1, replica_groups={{0,3},{1,2},{4,7},{5,6},{8,11},{9,10},{12,15},{13,14},{16,19},{17,18},{..., dimensions={0}, use_global_device_ids=true | all-gather | bytes 786432 | tf_op jit(solution)/shard_map/all_gather | solution.py:82
  95.3 0.1 dynamic-slice_add_fusion
  95.4 22.0 %all_to_all.23 = f32[8,64,128]{2,1,0:T(8,128)S(1)} all-to-all(f32[8,64,128]{2,1,0:T(8,128)S(1)} %bitcast.22), channel_id=1, replica_groups=mesh['x'=4,'y'=4,'parity'=8,'pair'=2,'core'=2] {'parity'}, dimensions={0} | all-to-all | bytes 524288 | tf_op jit(solution)/shard_map/all_to_all | solution.py:17
  117.4 27.6 %all_gather.19 = f32[1024,128]{1,0:T(8,128)S(1)} all-gather(f32[64,128]{1,0:T(8,128)S(1)} %sub.15), channel_id=1, replica_groups={{0,3,4,7,8,11,12,15,16,19,20,23,24,27,28,31},{1,2,5,6,9,10,13,14,17,18,..., dimensions={0}, use_global_device_ids=true | all-gather | bytes 557056 | tf_op jit(solution)/shard_map/all_gather | solution.py:87
  145.0 2.1 %collective-permute-start.1 = (f32[1024,128]{1,0:T(8,128)S(1)}, f32[1024,128]{1,0:T(8,128)S(1)}, u32[]{:S(2)}, u32[]{:S(2)}) collective-permute-start(f32[1024,128]{1,0:T(8,128)S(1)} %all_gather.19), channel_id=1, source_target_pairs={{0,1},{1,0},{2,3},{3,2},{4,5},{5,4},{6,7},{7,6},{8,9},{9,8},{10,11... | collective-permute-start | bytes 1572872 | tf_op jit(solution)/shard_map/ppermute | solution.py:88
  147.2 1.6 %collective-permute-done.1 = f32[1024,128]{1,0:T(8,128)S(1)} collective-permute-done((f32[1024,128]{1,0:T(8,128)S(1)}, f32[1024,128]{1,0:T(8,128)S(1)}, u32[]{:S(2)}, u32[]{:S(2)}) %collective-permute-start.1) | collective-permute-done | bytes 524320 | tf_op jit(solution)/shard_map/ppermute | solution.py:88
  148.8 1.1 maximum_select_fusion
  (19 shorter events, 0.3 us)
Async XLA Ops:
  1.7 16.8 %copy-start = (f32[2176,128]{1,0:T(8,128)S(1)}, f32[2176,128]{1,0:T(8,128)}, u32[]{:S(2)}) copy-start(f32[2176,128]{1,0:T(8,128)} %param.4) | copy-start | bytes 3342340
  18.5 47.6 %slice-start = ((f32[2304,128]{1,0:T(8,128)}), f32[128,128]{1,0:T(8,128)S(1)}, s32[]{:S(2)}) async-start(f32[2304,128]{1,0:T(8,128)} %param.3), calls=%async_computation.4 | async-start | bytes 131072 | tf_op jit(solution)/shard_map/slice | solution.py:46
  18.5 47.6 %copy-start.3 = (f32[2,64,128]{2,1,0:T(8,128)S(1)}, f32[2,64,128]{2,1,0:T(8,128)}, u32[]{:S(2)}) copy-start(f32[2,64,128]{2,1,0:T(8,128)} %param.5) | copy-start | bytes 196612
  79.8 0.7 copy-start.1
  80.5 4.2 %copy-start.2 = (f32[2304,128]{1,0:T(8,128)S(1)}, f32[2304,128]{1,0:T(8,128)}, u32[]{:S(2)}) copy-start(f32[2304,128]{1,0:T(8,128)} %param.3) | copy-start | bytes 3538948
  80.6 5.6 %collective-permute-start = (f32[1024,128]{1,0:T(8,128)S(1)}, f32[1024,128]{1,0:T(8,128)S(1)}, u32[]{:S(2)}, u32[]{:S(2)}) collective-permute-start(f32[1024,128]{1,0:T(8,128)S(1)} %get-tuple-element.20), channel_id=1, source_target_pairs={{0,1},{1,0},{2,3},{3,2},{4,5},{5,4},{6,7},{7,6},{8,9},{9,8},{10,11... | collective-permute-start | bytes 1572872 | tf_op jit(solution)/shard_map/ppermute | solution.py:77
  145.0 3.8 %collective-permute-start.1 = (f32[1024,128]{1,0:T(8,128)S(1)}, f32[1024,128]{1,0:T(8,128)S(1)}, u32[]{:S(2)}, u32[]{:S(2)}) collective-permute-start(f32[1024,128]{1,0:T(8,128)S(1)} %all_gather.19), channel_id=1, source_target_pairs={{0,1},{1,0},{2,3},{3,2},{4,5},{5,4},{6,7},{7,6},{8,9},{9,8},{10,11... | collective-permute-start | bytes 1572872 | tf_op jit(solution)/shard_map/ppermute | solution.py:88

commit v9 on v8

--- a/solution.py
+++ b/solution.py
@@ -51,12 +51,14 @@
     pair = lax.axis_index("pair")
     quarter = half // 2
     place = 2 * span_rows + side * half + lax.axis_index(Z) * rows
-    near_rows = span_rows // 2
-    near = lax.axis_index("core") * near_rows
-    starts = (side * half, (1 - side) * half, pair * quarter, (1 - pair) * quarter, near, place)
+    near_rows = span_rows // lax.axis_size(NEAR)
+    near = lax.axis_index(NEAR) * near_rows
+    kept_at, sent_at = span_rows + side * half, span_rows + (1 - side) * half
+    theirs_at = (1 - lax.axis_index("core")) * 2 * (factor.shape[1] // 2)
+    starts = (kept_at, sent_at, pair * quarter, (1 - pair) * quarter, near, place, theirs_at)
     first_part = product(inverses[0], first_rhs)
     first_part, second_rhs, starts = lax.optimization_barrier((first_part, second_rhs, starts))
-    half_kept, half_sent, quarter_kept, quarter_sent, near, place = starts
+    half_kept, half_sent, quarter_kept, quarter_sent, near, place, theirs_at = starts
 
     first_sol = taken_together(first_part, ROW)
     coupled = lax.optimization_barrier(product(factor[:span_rows, :span_cols], first_sol))
@@ -65,19 +67,22 @@
     coupled = lax.dynamic_slice(
         coupled, (0, near, 0), (coupled.shape[0], near_rows, coupled.shape[2]), allow_negative_indices=False
     )
-    coupled = taken_together(jnp.sum(coupled, axis=0), "parity")
-    coupled = lax.all_gather(coupled, "core", axis=0, tiled=True)
-    second_sol = taken_together(product(inverses[1], second_rhs - coupled), ROW)
+    coupled = jnp.sum(coupled, axis=0)
+    coupled = lax.all_gather(taken_together(coupled, "parity"), NEAR, axis=0, tiled=True)
+    second_part = product(inverses[1], second_rhs - coupled)
+    second_part, factor, rhs = lax.optimization_barrier((second_part, factor, rhs))
+    sent, kept = part_of(factor, half_sent, half), part_of(factor, half_kept, half)
+    came = lax.ppermute(sent, "core", SWAP)
+    trailing = part_of(rhs, place, rows)
+    second_sol = taken_together(second_part, ROW)
+    second_sol, kept, trailing = lax.optimization_barrier((second_sol, kept, trailing))
 
     both = lax.optimization_barrier(jnp.concatenate([first_sol, second_sol], 0))
-    terms = with_layout_constraint(product(factor[span_rows:], both, lax.Precision.HIGH), Layout((0, 1)))
-    terms = terms.reshape(2, spots // 2, 2, rows, -1).swapaxes(1, 2).reshape(2 * half, -1)
-    sent, kept = part_of(terms, half_sent, half), part_of(terms, half_kept, half)
-    sent, kept, rhs = lax.optimization_barrier((sent, kept, rhs))
-    taken = lax.ppermute(sent, "core", SWAP)
-    trailing = part_of(rhs, place, rows)
-    taken, trailing = lax.optimization_barrier((taken, trailing))
-    terms = kept + taken
+    all_both = lax.all_gather(both, "core", axis=0, tiled=True)
+    theirs = part_of(all_both, theirs_at, both.shape[0])
+    terms = product(kept, both, lax.Precision.HIGH) + product(came, theirs, lax.Precision.HIGH)
+    terms = with_layout_constraint(terms, Layout((0, 1)))
+    terms = terms.reshape(spots // 2, 2, rows, -1).swapaxes(0, 1).reshape(half, -1)
     sent, kept = part_of(terms, quarter_sent, quarter), part_of(terms, quarter_kept, quarter)
     sent = lax.all_gather(sent, NEAR, axis=0, tiled=True, axis_index_groups=CROSSED)
     taken = part_of(sent, quarter_sent, quarter)

time: 150 us -> 148 us (0.987)
  blocking collectives: 136 us -> 124 us
  waiting for transfers between devices: 3.13 us -> 9.62 us
  starting transfers between devices: 6.25 us -> 8.18 us
    all_to_all x4 -> x3, blocking collectives: 88.1 us -> 68.4 us  [exchanged(): return lax.all_to_all(blocks, axis, split_axis=0, concat_axis=0, tiled=True)]
    all_gather x1 -> x2, blocking collectives: 2.03 us -> 11.9 us  [the longest x1 8.44 us: local(): lax.all_gather(taken_together(coupled, 'parity'), NEAR, axis=0, tiled=True)]
    all_to_all x0 -> x1, waiting for transfers between devices: none -> 8.11 us  [exchanged(): return lax.all_to_all(blocks, axis, split_axis=0, concat_axis=0, tiled=True)]
    all_to_all x0 -> x1, starting transfers between devices: none -> 3.57 us  [exchanged(): return lax.all_to_all(blocks, axis, split_axis=0, concat_axis=0, tiled=True)]
    all_gather x1, blocking collectives: 27.6 us -> 25.6 us  [local(): lax.all_gather(trailing - terms, COL, axis=0, tiled=True, axis_index_grou...]
    ppermute x1, starting transfers between devices: 4.11 us -> 2.21 us  [local(): came = lax.ppermute(sent, 'core', SWAP)]
  transfers between devices with their start and end apart: 2 -> 3, of which waited for: 2 -> 2; matrix products, arithmetic and copies ran while one was open for 0% -> 0% of each run, Pallas kernels for 0% -> 0%
where the time goes in v9:
time: 148 us; the launch traced here: 147 us
  blocking collectives  124 us (84%)
  waiting for transfers between devices  9.62 us (6%)
  starting transfers between devices  8.18 us (6%)
  matrix products  2.25 us (2%)
    all_to_all x3, blocking collectives, exchanged(): return lax.all_to_all(blocks, axis, split_axis=0, concat_axis=0, tiled=True)  68.4 us
    all_gather x1, blocking collectives, local(): lax.all_gather(trailing - terms, COL, axis=0, tiled=True, axis_index_grou...  25.6 us
    all_gather x1, blocking collectives, local(): coupled = lax.all_gather(coupled, NEAR, axis=0)  9.24 us
    all_gather x1, blocking collectives, local(): lax.all_gather(sent, NEAR, axis=0, tiled=True, axis_index_groups=CROSSED)  8.95 us
    all_gather x1, blocking collectives, local(): lax.all_gather(taken_together(coupled, 'parity'), NEAR, axis=0, tiled=True)  8.44 us
    all_to_all x1, waiting for transfers between devices, exchanged(): return lax.all_to_all(blocks, axis, split_axis=0, concat_axis=0, tiled=True)  8.11 us
    all_to_all x1, starting transfers between devices, exchanged(): return lax.all_to_all(blocks, axis, split_axis=0, concat_axis=0, tiled=True)  3.57 us
    all_gather x1, blocking collectives, local(): all_both = lax.all_gather(both, 'core', axis=0, tiled=True)  3.48 us
  transfers between devices with their start and end apart: 3, of which 2 were waited for; matrix products, arithmetic and copies ran while one was open for 0% of the time, Pallas kernels for 0%

profile of v9, /device:TPU:1, one launch (start us, length us, event | category | flops | bytes accessed | tf_op | source)
XLA Modules:
  0.0 147.4 jit_solution(14407743131845043370)
XLA Ops:
  0.7 1.1 fusion.3
  1.9 0.0 slice-start
  1.9 16.7 %all_to_all.20 = f32[16,64,128]{2,1,0:T(8,128)S(1)} all-to-all(f32[16,64,128]{2,1,0:T(8,128)S(1)} %broadcast_in_dim.9), channel_id=1, replica_groups=mesh['x'=4,'y'=4,'parity'=8,'pair'=2,'core'=2] {'x','y'}, dimensions={0} | all-to-all | bytes 1048576 | tf_op jit(solution)/shard_map/all_to_all | solution.py:17
  18.7 0.2 convolution_bitcast_fusion
  18.9 9.2 %all-gather = f32[512,128]{1,0:T(8,128)S(1)} all-gather(f32[128,128]{1,0:T(8,128)S(1)} %convolution_bitcast_fusion), channel_id=2, replica_groups=mesh['x'=4,'y'=4,'parity'=8,'pair'=2,'core'=2] {'pair','core'}, dimensions={0}, use_global_device_ids=true | all-gather | bytes 327680 | tf_op jit(solution)/shard_map/all_gather | solution.py:66
  28.1 27.8 %all_to_all.21 = f32[8,32,128]{2,1,0:T(8,128)S(1)} all-to-all(f32[8,32,128]{2,1,0:T(8,128)S(1)} %broadcast_in_dim.10), channel_id=1, replica_groups=mesh['x'=4,'y'=4,'parity'=8,'pair'=2,'core'=2] {'parity'}, dimensions={0} | all-to-all | bytes 262144 | tf_op jit(solution)/shard_map/all_to_all | solution.py:17
  55.9 8.4 %all_gather.20 = f32[128,128]{1,0:T(8,128)S(1)} all-gather(f32[32,128]{1,0:T(8,128)S(1)} %reduce_sum.47), channel_id=1, replica_groups=mesh['x'=4,'y'=4,'parity'=8,'pair'=2,'core'=2] {'pair','core'}, dimensions={0}, use_global_device_ids=true | all-gather | bytes 81920 | tf_op jit(solution)/shard_map/all_gather | solution.py:71
  64.4 0.2 convolution_bitcast_fusion.1
  64.6 0.8 broadcast_in_dim.11
  65.4 3.6 %all-to-all-start.2 = ((f32[16,64,128]{2,1,0:T(8,128)}), f32[16,64,128]{2,1,0:T(8,128)S(1)}, u32[]{:S(2)}, u32[]{:S(2)}) async-start(f32[16,64,128]{2,1,0:T(8,128)} %broadcast_in_dim.11), calls=%async_computation.2 | async-start | bytes 1048576 | tf_op jit(solution)/shard_map/all_to_all | solution.py:17
  69.0 0.1 constant_dynamic-slice_fusion.1
  69.1 2.2 %collective-permute-start = (f32[1024,128]{1,0:T(8,128)S(1)}, f32[1024,128]{1,0:T(8,128)S(1)}, u32[]{:S(2)}, u32[]{:S(2)}) collective-permute-start(f32[1024,128]{1,0:T(8,128)S(1)} %get-tuple-element.32), channel_id=1, source_target_pairs={{0,1},{1,0},{2,3},{3,2},{4,5},{5,4},{6,7},{7,6},{8,9},{9,8},{10,11... | collective-permute-start | bytes 1572872 | tf_op jit(solution)/shard_map/ppermute | solution.py:75
  71.4 8.1 %all-to-all-done.2 = f32[16,64,128]{2,1,0:T(8,128)S(1)} async-done(((f32[16,64,128]{2,1,0:T(8,128)}), f32[16,64,128]{2,1,0:T(8,128)S(1)}, u32[]{:S(2)}, u32[]{:S(2)}) %all-to-all-start.2) | async-done | bytes 524320 | tf_op jit(solution)/shard_map/all_to_all | solution.py:17
  79.5 0.0 copy-start.1
  79.5 3.5 %all_gather.21 = f32[256,128]{1,0:T(8,128)S(1)} all-gather(f32[128,128]{1,0:T(8,128)S(1)} %pad_maximum_fusion), channel_id=1, replica_groups=mesh['x'=4,'y'=4,'parity'=8,'pair'=2,'core'=2] {'core'}, dimensions={0}, use_global_device_ids=true | all-gather | bytes 196608 | tf_op jit(solution)/shard_map/all_gather | solution.py:81
  83.0 0.4 fusion.10
  83.4 0.4 convolution_add_fusion
  83.9 8.9 %all_gather.22 = f32[1024,128]{1,0:T(8,128)S(1)} all-gather(f32[512,128]{1,0:T(8,128)S(1)} %constant_dynamic-slice_fusion), channel_id=1, replica_groups={{0,3},{1,2},{4,7},{5,6},{8,11},{9,10},{12,15},{13,14},{16,19},{17,18},{..., dimensions={0}, use_global_device_ids=true | all-gather | bytes 786432 | tf_op jit(solution)/shard_map/all_gather | solution.py:87
  92.8 0.1 dynamic-slice_add_fusion
  92.9 23.9 %all_to_all.22 = f32[8,64,128]{2,1,0:T(8,128)S(1)} all-to-all(f32[8,64,128]{2,1,0:T(8,128)S(1)} %bitcast.23), channel_id=1, replica_groups=mesh['x'=4,'y'=4,'parity'=8,'pair'=2,'core'=2] {'parity'}, dimensions={0} | all-to-all | bytes 524288 | tf_op jit(solution)/shard_map/all_to_all | solution.py:17
  116.8 25.6 %all_gather.23 = f32[1024,128]{1,0:T(8,128)S(1)} all-gather(f32[64,128]{1,0:T(8,128)S(1)} %sub.19), channel_id=1, replica_groups={{0,3,4,7,8,11,12,15,16,19,20,23,24,27,28,31},{1,2,5,6,9,10,13,14,17,18,..., dimensions={0}, use_global_device_ids=true | all-gather | bytes 557056 | tf_op jit(solution)/shard_map/all_gather | solution.py:92
  142.4 2.4 %collective-permute-start.1 = (f32[1024,128]{1,0:T(8,128)S(1)}, f32[1024,128]{1,0:T(8,128)S(1)}, u32[]{:S(2)}, u32[]{:S(2)}) collective-permute-start(f32[1024,128]{1,0:T(8,128)S(1)} %all_gather.23), channel_id=1, source_target_pairs={{0,1},{1,0},{2,3},{3,2},{4,5},{5,4},{6,7},{7,6},{8,9},{9,8},{10,11... | collective-permute-start | bytes 1572872 | tf_op jit(solution)/shard_map/ppermute | solution.py:93
  144.8 1.5 %collective-permute-done.1 = f32[1024,128]{1,0:T(8,128)S(1)} collective-permute-done((f32[1024,128]{1,0:T(8,128)S(1)}, f32[1024,128]{1,0:T(8,128)S(1)}, u32[]{:S(2)}, u32[]{:S(2)}) %collective-permute-start.1) | collective-permute-done | bytes 524320 | tf_op jit(solution)/shard_map/ppermute | solution.py:93
  146.3 1.1 maximum_select_fusion
  (21 shorter events, 0.3 us)
Async XLA Ops:
  0.6 18.0 %copy-start = (f32[2176,128]{1,0:T(8,128)S(1)}, f32[2176,128]{1,0:T(8,128)}, u32[]{:S(2)}) copy-start(f32[2176,128]{1,0:T(8,128)} %param.4) | copy-start | bytes 3342340
  1.9 62.5 %slice-start = ((f32[2304,128]{1,0:T(8,128)}), f32[128,128]{1,0:T(8,128)S(1)}, s32[]{:S(2)}) async-start(f32[2304,128]{1,0:T(8,128)} %param.3), calls=%async_computation.4 | async-start | bytes 131072 | tf_op jit(solution)/shard_map/slice | solution.py:46
  1.9 62.5 %copy-start.3 = (f32[2,64,128]{2,1,0:T(8,128)S(1)}, f32[2,64,128]{2,1,0:T(8,128)}, u32[]{:S(2)}) copy-start(f32[2,64,128]{2,1,0:T(8,128)} %param.5) | copy-start | bytes 196612
  65.4 14.1 %all-to-all-start.2 = ((f32[16,64,128]{2,1,0:T(8,128)}), f32[16,64,128]{2,1,0:T(8,128)S(1)}, u32[]{:S(2)}, u32[]{:S(2)}) async-start(f32[16,64,128]{2,1,0:T(8,128)} %broadcast_in_dim.11), calls=%async_computation.2 | async-start | bytes 1048576 | tf_op jit(solution)/shard_map/all_to_all | solution.py:17
  69.0 2.3 %copy-start.2 = (f32[2304,128]{1,0:T(8,128)S(1)}, f32[2304,128]{1,0:T(8,128)}, u32[]{:S(2)}) copy-start(f32[2304,128]{1,0:T(8,128)} %param.3) | copy-start | bytes 3538948
  69.1 14.3 %collective-permute-start = (f32[1024,128]{1,0:T(8,128)S(1)}, f32[1024,128]{1,0:T(8,128)S(1)}, u32[]{:S(2)}, u32[]{:S(2)}) collective-permute-start(f32[1024,128]{1,0:T(8,128)S(1)} %get-tuple-element.32), channel_id=1, source_target_pairs={{0,1},{1,0},{2,3},{3,2},{4,5},{5,4},{6,7},{7,6},{8,9},{9,8},{10,11... | collective-permute-start | bytes 1572872 | tf_op jit(solution)/shard_map/ppermute | solution.py:75
  79.5 4.3 %copy-start.1 = (f32[128,128]{1,0:T(8,128)}, f32[128,128]{1,0:T(8,128)S(1)}, u32[]{:S(2)}) copy-start(f32[128,128]{1,0:T(8,128)S(1)} %pad_maximum_fusion) | copy-start | bytes 196612
  142.4 3.9 %collective-permute-start.1 = (f32[1024,128]{1,0:T(8,128)S(1)}, f32[1024,128]{1,0:T(8,128)S(1)}, u32[]{:S(2)}, u32[]{:S(2)}) collective-permute-start(f32[1024,128]{1,0:T(8,128)S(1)} %all_gather.23), channel_id=1, source_target_pairs={{0,1},{1,0},{2,3},{3,2},{4,5},{5,4},{6,7},{7,6},{8,9},{9,8},{10,11... | collective-permute-start | bytes 1572872 | tf_op jit(solution)/shard_map/ppermute | solution.py:93

commit v10 on v9

--- a/solution.py
+++ b/solution.py
@@ -10,7 +10,6 @@
 Z = ("parity", "pair")
 COL = (*Z, "core")
 SWAP = [(0, 1), (1, 0)]
-CROSSED = [[0, 3], [1, 2]]
 
 
 def exchanged(blocks, axis):
@@ -39,6 +38,12 @@
     return lax.dynamic_slice(array, (start, 0), (rows, array.shape[1]), allow_negative_indices=False)
 
 
+def quarter_of(blocks, first, pair):
+    sizes = (blocks.shape[0] // 2, 1, *blocks.shape[2:])
+    part = lax.dynamic_slice(blocks, (first, pair, 0, 0), sizes, allow_negative_indices=False)
+    return part.reshape(-1, blocks.shape[-1])
+
+
 def local(rhs, factor, inverses):
     span_rows = inverses.shape[2]
     span_cols = factor.shape[1] // 2
@@ -49,16 +54,26 @@
     half = spots * rows
     side = lax.axis_index("core") ^ lax.axis_index("pair")
     pair = lax.axis_index("pair")
-    quarter = half // 2
     place = 2 * span_rows + side * half + lax.axis_index(Z) * rows
     near_rows = span_rows // lax.axis_size(NEAR)
     near = lax.axis_index(NEAR) * near_rows
-    kept_at, sent_at = span_rows + side * half, span_rows + (1 - side) * half
-    theirs_at = (1 - lax.axis_index("core")) * 2 * (factor.shape[1] // 2)
-    starts = (kept_at, sent_at, pair * quarter, (1 - pair) * quarter, near, place, theirs_at)
+    core, other_core = lax.axis_index("core"), 1 - lax.axis_index("core")
+    other_pair, group = 1 - pair, spots // 2
+    unknowns = factor.shape[1]
+    starts = (
+        1 + side * group,
+        1 + (1 - side) * group,
+        pair,
+        other_pair,
+        near,
+        place,
+        (pair * 2 + other_core) * unknowns,
+        (other_pair * 2 + other_core) * unknowns,
+        (other_pair * 2 + core) * unknowns,
+    )
     first_part = product(inverses[0], first_rhs)
     first_part, second_rhs, starts = lax.optimization_barrier((first_part, second_rhs, starts))
-    half_kept, half_sent, quarter_kept, quarter_sent, near, place, theirs_at = starts
+    blocks_at, other_at, pair, other_pair, near, place, across_at, crossed_at, straight_at = starts
 
     first_sol = taken_together(first_part, ROW)
     coupled = lax.optimization_barrier(product(factor[:span_rows, :span_cols], first_sol))
@@ -71,22 +86,24 @@
     coupled = lax.all_gather(taken_together(coupled, "parity"), NEAR, axis=0, tiled=True)
     second_part = product(inverses[1], second_rhs - coupled)
     second_part, factor, rhs = lax.optimization_barrier((second_part, factor, rhs))
-    sent, kept = part_of(factor, half_sent, half), part_of(factor, half_kept, half)
-    came = lax.ppermute(sent, "core", SWAP)
+    blocks = factor.reshape(-1, 2, rows, factor.shape[1])
+    own = quarter_of(blocks, blocks_at, pair)
+    across = quarter_of(blocks, other_at, pair)
+    crossed = quarter_of(blocks, blocks_at, other_pair)
+    straight = quarter_of(blocks, other_at, other_pair)
+    across = lax.ppermute(across, NEAR, [(0, 1), (1, 0), (2, 3), (3, 2)])
+    crossed = lax.ppermute(crossed, NEAR, [(0, 3), (3, 0), (1, 2), (2, 1)])
+    straight = lax.ppermute(straight, NEAR, [(0, 2), (2, 0), (1, 3), (3, 1)])
     trailing = part_of(rhs, place, rows)
     second_sol = taken_together(second_part, ROW)
-    second_sol, kept, trailing = lax.optimization_barrier((second_sol, kept, trailing))
+    second_sol, own, trailing = lax.optimization_barrier((second_sol, own, trailing))
 
     both = lax.optimization_barrier(jnp.concatenate([first_sol, second_sol], 0))
-    all_both = lax.all_gather(both, "core", axis=0, tiled=True)
-    theirs = part_of(all_both, theirs_at, both.shape[0])
-    terms = product(kept, both, lax.Precision.HIGH) + product(came, theirs, lax.Precision.HIGH)
-    terms = with_layout_constraint(terms, Layout((0, 1)))
-    terms = terms.reshape(spots // 2, 2, rows, -1).swapaxes(0, 1).reshape(half, -1)
-    sent, kept = part_of(terms, quarter_sent, quarter), part_of(terms, quarter_kept, quarter)
-    sent = lax.all_gather(sent, NEAR, axis=0, tiled=True, axis_index_groups=CROSSED)
-    taken = part_of(sent, quarter_sent, quarter)
-    terms = my_sum(kept + taken, "parity")
+    near_both = lax.all_gather(both, NEAR, axis=0, tiled=True)
+    terms = product(own, both, lax.Precision.HIGH)
+    for part, at in ((across, across_at), (crossed, crossed_at), (straight, straight_at)):
+        terms = terms + product(part, part_of(near_both, at, both.shape[0]), lax.Precision.HIGH)
+    terms = my_sum(with_layout_constraint(terms, Layout((0, 1))), "parity")
 
     rings = [[2 * z + (z + start) % 2 for z in range(spots)] for start in range(2)]
     mine = lax.all_gather(trailing - terms, COL, axis=0, tiled=True, axis_index_groups=rings)

time: 148 us -> 144 us (0.973)
  waiting for transfers between devices: 9.62 us -> 4.3 us
  starting transfers between devices: 8.18 us -> 13.3 us
  blocking collectives: 124 us -> 120 us
    all_to_all x1, waiting for transfers between devices: 8.11 us -> 2.57 us  [exchanged(): return lax.all_to_all(blocks, axis, split_axis=0, concat_axis=0, tiled=True)]
    ppermute x1 -> x3, starting transfers between devices: 2.21 us -> 7.72 us  [the longest x1 3.17 us: local(): crossed = lax.ppermute(crossed, NEAR, [(0, 3), (3, 0), (1, 2), (2, 1)])]
    all_gather x2 -> x1, blocking collectives: 12.4 us -> 7.78 us  [local(): near_both = lax.all_gather(both, NEAR, axis=0, tiled=True)]
  transfers between devices with their start and end apart: 3 -> 5, of which waited for: 2 -> 2; matrix products, arithmetic and copies ran while one was open for 0% -> 1% of each run, Pallas kernels for 0% -> 0%
where the time goes in v10:
time: 144 us; the launch traced here: 143 us
  blocking collectives  120 us (83%)
  starting transfers between devices  13.3 us (9%)
  waiting for transfers between devices  4.3 us (3%)
  matrix products  2.55 us (2%)
    all_to_all x3, blocking collectives, exchanged(): return lax.all_to_all(blocks, axis, split_axis=0, concat_axis=0, tiled=True)  67.6 us
    all_gather x1, blocking collectives, local(): lax.all_gather(trailing - terms, COL, axis=0, tiled=True, axis_index_grou...  26.7 us
    all_gather x1, blocking collectives, local(): coupled = lax.all_gather(coupled, NEAR, axis=0)  9.24 us
    all_gather x1, blocking collectives, local(): lax.all_gather(taken_together(coupled, 'parity'), NEAR, axis=0, tiled=True)  8.44 us
    all_gather x1, blocking collectives, local(): near_both = lax.all_gather(both, NEAR, axis=0, tiled=True)  7.78 us
    all_to_all x1, starting transfers between devices, exchanged(): return lax.all_to_all(blocks, axis, split_axis=0, concat_axis=0, tiled=True)  3.57 us
    ppermute x1, starting transfers between devices, local(): crossed = lax.ppermute(crossed, NEAR, [(0, 3), (3, 0), (1, 2), (2, 1)])  3.17 us
  transfers between devices with their start and end apart: 5, of which 2 were waited for; matrix products, arithmetic and copies ran while one was open for 1% of the time, Pallas kernels for 0%

profile of v10, /device:TPU:1, one launch (start us, length us, event | category | flops | bytes accessed | tf_op | source)
XLA Modules:
  0.0 143.1 jit_solution(9253108792719835635)
XLA Ops:
  0.7 1.1 fusion.7
  1.9 16.7 %all_to_all.20 = f32[16,64,128]{2,1,0:T(8,128)S(1)} all-to-all(f32[16,64,128]{2,1,0:T(8,128)S(1)} %broadcast_in_dim.9), channel_id=1, replica_groups=mesh['x'=4,'y'=4,'parity'=8,'pair'=2,'core'=2] {'x','y'}, dimensions={0} | all-to-all | bytes 1048576 | tf_op jit(solution)/shard_map/all_to_all | solution.py:16
  18.7 0.2 convolution_bitcast_fusion
  18.9 9.2 %all-gather = f32[512,128]{1,0:T(8,128)S(1)} all-gather(f32[128,128]{1,0:T(8,128)S(1)} %convolution_bitcast_fusion), channel_id=2, replica_groups=mesh['x'=4,'y'=4,'parity'=8,'pair'=2,'core'=2] {'pair','core'}, dimensions={0}, use_global_device_ids=true | all-gather | bytes 327680 | tf_op jit(solution)/shard_map/all_gather | solution.py:81
  28.1 27.8 %all_to_all.21 = f32[8,32,128]{2,1,0:T(8,128)S(1)} all-to-all(f32[8,32,128]{2,1,0:T(8,128)S(1)} %broadcast_in_dim.10), channel_id=1, replica_groups=mesh['x'=4,'y'=4,'parity'=8,'pair'=2,'core'=2] {'parity'}, dimensions={0} | all-to-all | bytes 262144 | tf_op jit(solution)/shard_map/all_to_all | solution.py:16
  55.9 8.4 %all_gather.17 = f32[128,128]{1,0:T(8,128)S(1)} all-gather(f32[32,128]{1,0:T(8,128)S(1)} %reduce_sum.47), channel_id=1, replica_groups=mesh['x'=4,'y'=4,'parity'=8,'pair'=2,'core'=2] {'pair','core'}, dimensions={0}, use_global_device_ids=true | all-gather | bytes 81920 | tf_op jit(solution)/shard_map/all_gather | solution.py:86
  64.4 0.2 convolution_bitcast_fusion.1
  64.6 0.8 broadcast_in_dim.11
  65.4 3.6 %all-to-all-start.2 = ((f32[16,64,128]{2,1,0:T(8,128)}), f32[16,64,128]{2,1,0:T(8,128)S(1)}, u32[]{:S(2)}, u32[]{:S(2)}) async-start(f32[16,64,128]{2,1,0:T(8,128)} %broadcast_in_dim.11), calls=%async_computation.2 | async-start | bytes 1048576 | tf_op jit(solution)/shard_map/all_to_all | solution.py:16
  69.0 0.1 constant_dynamic-slice_fusion.1
  69.1 2.6 %collective-permute-start.2 = (f32[512,128]{1,0:T(8,128)S(1)}, f32[512,128]{1,0:T(8,128)S(1)}, u32[]{:S(2)}, u32[]{:S(2)}) collective-permute-start(f32[512,128]{1,0:T(8,128)S(1)} %bitcast.29), channel_id=1, source_target_pairs={{0,2},{2,0},{1,3},{3,1},{4,6},{6,4},{5,7},{7,5},{8,10},{10,8},{9,1... | collective-permute-start | bytes 786440 | tf_op jit(solution)/shard_map/ppermute | solution.py:96
  71.7 3.2 %collective-permute-start.1 = (f32[512,128]{1,0:T(8,128)S(1)}, f32[512,128]{1,0:T(8,128)S(1)}, u32[]{:S(2)}, u32[]{:S(2)}) collective-permute-start(f32[512,128]{1,0:T(8,128)S(1)} %bitcast.27), channel_id=1, source_target_pairs={{0,3},{3,0},{1,2},{2,1},{4,7},{7,4},{5,6},{6,5},{8,11},{11,8},{9,1... | collective-permute-start | bytes 786440 | tf_op jit(solution)/shard_map/ppermute | solution.py:95
  74.9 2.0 %collective-permute-start = (f32[512,128]{1,0:T(8,128)S(1)}, f32[512,128]{1,0:T(8,128)S(1)}, u32[]{:S(2)}, u32[]{:S(2)}) collective-permute-start(f32[512,128]{1,0:T(8,128)S(1)} %bitcast.28), channel_id=1, source_target_pairs={{0,1},{1,0},{2,3},{3,2},{4,5},{5,4},{6,7},{7,6},{8,9},{9,8},{10,11... | collective-permute-start | bytes 786440 | tf_op jit(solution)/shard_map/ppermute | solution.py:94
  76.9 2.6 %all-to-all-done.2 = f32[16,64,128]{2,1,0:T(8,128)S(1)} async-done(((f32[16,64,128]{2,1,0:T(8,128)}), f32[16,64,128]{2,1,0:T(8,128)S(1)}, u32[]{:S(2)}, u32[]{:S(2)}) %all-to-all-start.2) | async-done | bytes 524320 | tf_op jit(solution)/shard_map/all_to_all | solution.py:16
  79.5 0.3 fusion.16
  79.8 7.8 %all_gather.18 = f32[512,128]{1,0:T(8,128)S(1)} all-gather(f32[128,128]{1,0:T(8,128)S(1)} %pad_maximum_fusion), channel_id=1, replica_groups=mesh['x'=4,'y'=4,'parity'=8,'pair'=2,'core'=2] {'pair','core'}, dimensions={0}, use_global_device_ids=true | all-gather | bytes 327680 | tf_op jit(solution)/shard_map/all_gather | solution.py:102
  87.6 0.3 fusion.1
  87.9 0.3 convolution_add_fusion.1
  88.2 0.3 fusion
  88.4 23.0 %all_to_all.22 = f32[8,64,128]{2,1,0:T(8,128)S(1)} all-to-all(f32[8,64,128]{2,1,0:T(8,128)S(1)} %bitcast.25), channel_id=1, replica_groups=mesh['x'=4,'y'=4,'parity'=8,'pair'=2,'core'=2] {'parity'}, dimensions={0} | all-to-all | bytes 524288 | tf_op jit(solution)/shard_map/all_to_all | solution.py:16
  111.5 26.7 %all_gather.19 = f32[1024,128]{1,0:T(8,128)S(1)} all-gather(f32[64,128]{1,0:T(8,128)S(1)} %sub.19), channel_id=1, replica_groups={{0,3,4,7,8,11,12,15,16,19,20,23,24,27,28,31},{1,2,5,6,9,10,13,14,17,18,..., dimensions={0}, use_global_device_ids=true | all-gather | bytes 557056 | tf_op jit(solution)/shard_map/all_gather | solution.py:109
  138.2 2.1 %collective-permute-start.3 = (f32[1024,128]{1,0:T(8,128)S(1)}, f32[1024,128]{1,0:T(8,128)S(1)}, u32[]{:S(2)}, u32[]{:S(2)}) collective-permute-start(f32[1024,128]{1,0:T(8,128)S(1)} %all_gather.19), channel_id=1, source_target_pairs={{0,1},{1,0},{2,3},{3,2},{4,5},{5,4},{6,7},{7,6},{8,9},{9,8},{10,11... | collective-permute-start | bytes 1572872 | tf_op jit(solution)/shard_map/ppermute | solution.py:110
  140.2 1.7 %collective-permute-done.3 = f32[1024,128]{1,0:T(8,128)S(1)} collective-permute-done((f32[1024,128]{1,0:T(8,128)S(1)}, f32[1024,128]{1,0:T(8,128)S(1)}, u32[]{:S(2)}, u32[]{:S(2)}) %collective-permute-start.3) | collective-permute-done | bytes 524320 | tf_op jit(solution)/shard_map/ppermute | solution.py:110
  142.0 1.1 maximum_select_fusion
  (23 shorter events, 0.2 us)
Async XLA Ops:
  0.7 18.0 %copy-start = (f32[2176,128]{1,0:T(8,128)S(1)}, f32[2176,128]{1,0:T(8,128)}, u32[]{:S(2)}) copy-start(f32[2176,128]{1,0:T(8,128)} %param.4) | copy-start | bytes 3342340
  1.9 62.5 %slice-start = ((f32[2304,128]{1,0:T(8,128)}), f32[128,128]{1,0:T(8,128)S(1)}, s32[]{:S(2)}) async-start(f32[2304,128]{1,0:T(8,128)} %param.3), calls=%async_computation.4 | async-start | bytes 131072 | tf_op jit(solution)/shard_map/slice | solution.py:51
  1.9 62.5 %copy-start.3 = (f32[2,64,128]{2,1,0:T(8,128)S(1)}, f32[2,64,128]{2,1,0:T(8,128)}, u32[]{:S(2)}) copy-start(f32[2,64,128]{2,1,0:T(8,128)} %param.5) | copy-start | bytes 196612
  65.4 14.1 %all-to-all-start.2 = ((f32[16,64,128]{2,1,0:T(8,128)}), f32[16,64,128]{2,1,0:T(8,128)S(1)}, u32[]{:S(2)}, u32[]{:S(2)}) async-start(f32[16,64,128]{2,1,0:T(8,128)} %broadcast_in_dim.11), calls=%async_computation.2 | async-start | bytes 1048576 | tf_op jit(solution)/shard_map/all_to_all | solution.py:16
  69.0 7.9 %copy-start.2 = (f32[2304,128]{1,0:T(8,128)S(1)}, f32[2304,128]{1,0:T(8,128)}, u32[]{:S(2)}) copy-start(f32[2304,128]{1,0:T(8,128)} %param.3) | copy-start | bytes 3538948
  69.1 18.4 %collective-permute-start.2 = (f32[512,128]{1,0:T(8,128)S(1)}, f32[512,128]{1,0:T(8,128)S(1)}, u32[]{:S(2)}, u32[]{:S(2)}) collective-permute-start(f32[512,128]{1,0:T(8,128)S(1)} %bitcast.29), channel_id=1, source_target_pairs={{0,2},{2,0},{1,3},{3,1},{4,6},{6,4},{5,7},{7,5},{8,10},{10,8},{9,1... | collective-permute-start | bytes 786440 | tf_op jit(solution)/shard_map/ppermute | solution.py:96
  71.7 16.4 %collective-permute-start.1 = (f32[512,128]{1,0:T(8,128)S(1)}, f32[512,128]{1,0:T(8,128)S(1)}, u32[]{:S(2)}, u32[]{:S(2)}) collective-permute-start(f32[512,128]{1,0:T(8,128)S(1)} %bitcast.27), channel_id=1, source_target_pairs={{0,3},{3,0},{1,2},{2,1},{4,7},{7,4},{5,6},{6,5},{8,11},{11,8},{9,1... | collective-permute-start | bytes 786440 | tf_op jit(solution)/shard_map/ppermute | solution.py:95
  74.9 12.9 %collective-permute-start = (f32[512,128]{1,0:T(8,128)S(1)}, f32[512,128]{1,0:T(8,128)S(1)}, u32[]{:S(2)}, u32[]{:S(2)}) collective-permute-start(f32[512,128]{1,0:T(8,128)S(1)} %bitcast.28), channel_id=1, source_target_pairs={{0,1},{1,0},{2,3},{3,2},{4,5},{5,4},{6,7},{7,6},{8,9},{9,8},{10,11... | collective-permute-start | bytes 786440 | tf_op jit(solution)/shard_map/ppermute | solution.py:94
  79.5 8.6 %copy-start.1 = (f32[128,128]{1,0:T(8,128)}, f32[128,128]{1,0:T(8,128)S(1)}, u32[]{:S(2)}) copy-start(f32[128,128]{1,0:T(8,128)S(1)} %pad_maximum_fusion) | copy-start | bytes 196612
  138.2 3.8 %collective-permute-start.3 = (f32[1024,128]{1,0:T(8,128)S(1)}, f32[1024,128]{1,0:T(8,128)S(1)}, u32[]{:S(2)}, u32[]{:S(2)}) collective-permute-start(f32[1024,128]{1,0:T(8,128)S(1)} %all_gather.19), channel_id=1, source_target_pairs={{0,1},{1,0},{2,3},{3,2},{4,5},{5,4},{6,7},{7,6},{8,9},{9,8},{10,11... | collective-permute-start | bytes 1572872 | tf_op jit(solution)/shard_map/ppermute | solution.py:110

commit v11 on v10

--- a/solution.py
+++ b/solution.py
@@ -100,9 +100,9 @@
 
     both = lax.optimization_barrier(jnp.concatenate([first_sol, second_sol], 0))
     near_both = lax.all_gather(both, NEAR, axis=0, tiled=True)
-    terms = product(own, both, lax.Precision.HIGH)
-    for part, at in ((across, across_at), (crossed, crossed_at), (straight, straight_at)):
-        terms = terms + product(part, part_of(near_both, at, both.shape[0]), lax.Precision.HIGH)
+    theirs = [part_of(near_both, at, both.shape[0]) for at in (across_at, crossed_at, straight_at)]
+    columns = jnp.concatenate([own, across, crossed, straight], 1)
+    terms = product(columns, jnp.concatenate([both, *theirs], 0), lax.Precision.HIGH)
     terms = my_sum(with_layout_constraint(terms, Layout((0, 1))), "parity")
 
     rings = [[2 * z + (z + start) % 2 for z in range(spots)] for start in range(2)]

time: 144 us -> 143 us (level)
  transfers between devices with their start and end apart: 5 -> 5, of which waited for: 2 -> 2; matrix products, arithmetic and copies ran while one was open for 1% -> 0% of each run, Pallas kernels for 0% -> 0%
where the time goes in v11:
time: 143 us
  blocking collectives  120 us (84%)
  starting transfers between devices  13.5 us (9%)
  waiting for transfers between devices  4.16 us (3%)
  matrix products  2.11 us (1%)
    all_to_all x3, blocking collectives, exchanged(): return lax.all_to_all(blocks, axis, split_axis=0, concat_axis=0, tiled=True)  68.3 us
    all_gather x1, blocking collectives, local(): lax.all_gather(trailing - terms, COL, axis=0, tiled=True, axis_index_grou...  25.8 us
    all_gather x1, blocking collectives, local(): coupled = lax.all_gather(coupled, NEAR, axis=0)  9.24 us
    all_gather x1, blocking collectives, local(): lax.all_gather(taken_together(coupled, 'parity'), NEAR, axis=0, tiled=True)  8.44 us
    all_gather x1, blocking collectives, local(): near_both = lax.all_gather(both, NEAR, axis=0, tiled=True)  8.04 us
    all_to_all x1, starting transfers between devices, exchanged(): return lax.all_to_all(blocks, axis, split_axis=0, concat_axis=0, tiled=True)  3.57 us
    ppermute x1, starting transfers between devices, local(): crossed = lax.ppermute(crossed, NEAR, [(0, 3), (3, 0), (1, 2), (2, 1)])  2.95 us
  transfers between devices with their start and end apart: 5, of which 2 were waited for; matrix products, arithmetic and copies ran while one was open for 0% of the time, Pallas kernels for 0%

profile of v11, /device:TPU:1, one launch (start us, length us, event | category | flops | bytes accessed | tf_op | source)
XLA Modules:
  0.0 142.8 jit_solution(4184857471511900030)
XLA Ops:
  0.7 1.1 fusion.17
  1.9 0.0 slice-start
  1.9 0.0 copy-start.3
  1.9 16.7 %all_to_all.20 = f32[16,64,128]{2,1,0:T(8,128)S(1)} all-to-all(f32[16,64,128]{2,1,0:T(8,128)S(1)} %broadcast_in_dim.9), channel_id=1, replica_groups=mesh['x'=4,'y'=4,'parity'=8,'pair'=2,'core'=2] {'x','y'}, dimensions={0} | all-to-all | bytes 1048576 | tf_op jit(solution)/shard_map/all_to_all | solution.py:16
  18.7 0.2 convolution_bitcast_fusion
  18.9 9.2 %all-gather = f32[512,128]{1,0:T(8,128)S(1)} all-gather(f32[128,128]{1,0:T(8,128)S(1)} %convolution_bitcast_fusion), channel_id=2, replica_groups=mesh['x'=4,'y'=4,'parity'=8,'pair'=2,'core'=2] {'pair','core'}, dimensions={0}, use_global_device_ids=true | all-gather | bytes 327680 | tf_op jit(solution)/shard_map/all_gather | solution.py:81
  28.1 27.8 %all_to_all.21 = f32[8,32,128]{2,1,0:T(8,128)S(1)} all-to-all(f32[8,32,128]{2,1,0:T(8,128)S(1)} %broadcast_in_dim.10), channel_id=1, replica_groups=mesh['x'=4,'y'=4,'parity'=8,'pair'=2,'core'=2] {'parity'}, dimensions={0} | all-to-all | bytes 262144 | tf_op jit(solution)/shard_map/all_to_all | solution.py:16
  55.9 8.4 %all_gather.17 = f32[128,128]{1,0:T(8,128)S(1)} all-gather(f32[32,128]{1,0:T(8,128)S(1)} %reduce_sum.47), channel_id=1, replica_groups=mesh['x'=4,'y'=4,'parity'=8,'pair'=2,'core'=2] {'pair','core'}, dimensions={0}, use_global_device_ids=true | all-gather | bytes 81920 | tf_op jit(solution)/shard_map/all_gather | solution.py:86
  64.4 0.2 convolution_bitcast_fusion.1
  64.6 0.8 broadcast_in_dim.11
  65.4 3.6 %all-to-all-start.2 = ((f32[16,64,128]{2,1,0:T(8,128)}), f32[16,64,128]{2,1,0:T(8,128)S(1)}, u32[]{:S(2)}, u32[]{:S(2)}) async-start(f32[16,64,128]{2,1,0:T(8,128)} %broadcast_in_dim.11), calls=%async_computation.2 | async-start | bytes 1048576 | tf_op jit(solution)/shard_map/all_to_all | solution.py:16
  69.0 0.1 constant_dynamic-slice_fusion.5
  69.1 2.4 %collective-permute-start.2 = (f32[512,128]{1,0:T(8,128)S(1)}, f32[512,128]{1,0:T(8,128)S(1)}, u32[]{:S(2)}, u32[]{:S(2)}) collective-permute-start(f32[512,128]{1,0:T(8,128)S(1)} %bitcast.23), channel_id=1, source_target_pairs={{0,2},{2,0},{1,3},{3,1},{4,6},{6,4},{5,7},{7,5},{8,10},{10,8},{9,1... | collective-permute-start | bytes 786440 | tf_op jit(solution)/shard_map/ppermute | solution.py:96
  71.6 2.4 %collective-permute-start = (f32[512,128]{1,0:T(8,128)S(1)}, f32[512,128]{1,0:T(8,128)S(1)}, u32[]{:S(2)}, u32[]{:S(2)}) collective-permute-start(f32[512,128]{1,0:T(8,128)S(1)} %bitcast.22), channel_id=1, source_target_pairs={{0,1},{1,0},{2,3},{3,2},{4,5},{5,4},{6,7},{7,6},{8,9},{9,8},{10,11... | collective-permute-start | bytes 786440 | tf_op jit(solution)/shard_map/ppermute | solution.py:94
  73.9 3.0 %collective-permute-start.1 = (f32[512,128]{1,0:T(8,128)S(1)}, f32[512,128]{1,0:T(8,128)S(1)}, u32[]{:S(2)}, u32[]{:S(2)}) collective-permute-start(f32[512,128]{1,0:T(8,128)S(1)} %bitcast.21), channel_id=1, source_target_pairs={{0,3},{3,0},{1,2},{2,1},{4,7},{7,4},{5,6},{6,5},{8,11},{11,8},{9,1... | collective-permute-start | bytes 786440 | tf_op jit(solution)/shard_map/ppermute | solution.py:95
  76.9 2.6 %all-to-all-done.2 = f32[16,64,128]{2,1,0:T(8,128)S(1)} async-done(((f32[16,64,128]{2,1,0:T(8,128)}), f32[16,64,128]{2,1,0:T(8,128)S(1)}, u32[]{:S(2)}, u32[]{:S(2)}) %all-to-all-start.2) | async-done | bytes 524320 | tf_op jit(solution)/shard_map/all_to_all | solution.py:16
  79.5 0.0 copy-start.1
  79.5 8.0 %all_gather.18 = f32[512,128]{1,0:T(8,128)S(1)} all-gather(f32[128,128]{1,0:T(8,128)S(1)} %pad_maximum_fusion), channel_id=1, replica_groups=mesh['x'=4,'y'=4,'parity'=8,'pair'=2,'core'=2] {'pair','core'}, dimensions={0}, use_global_device_ids=true | all-gather | bytes 327680 | tf_op jit(solution)/shard_map/all_gather | solution.py:102
  87.6 0.6 fusion
  88.3 23.8 %all_to_all.22 = f32[8,64,128]{2,1,0:T(8,128)S(1)} all-to-all(f32[8,64,128]{2,1,0:T(8,128)S(1)} %bitcast.24), channel_id=1, replica_groups=mesh['x'=4,'y'=4,'parity'=8,'pair'=2,'core'=2] {'parity'}, dimensions={0} | all-to-all | bytes 524288 | tf_op jit(solution)/shard_map/all_to_all | solution.py:16
  112.1 25.8 %all_gather.19 = f32[1024,128]{1,0:T(8,128)S(1)} all-gather(f32[64,128]{1,0:T(8,128)S(1)} %sub.19), channel_id=1, replica_groups={{0,3,4,7,8,11,12,15,16,19,20,23,24,27,28,31},{1,2,5,6,9,10,13,14,17,18,..., dimensions={0}, use_global_device_ids=true | all-gather | bytes 557056 | tf_op jit(solution)/shard_map/all_gather | solution.py:109
  137.9 2.2 %collective-permute-start.3 = (f32[1024,128]{1,0:T(8,128)S(1)}, f32[1024,128]{1,0:T(8,128)S(1)}, u32[]{:S(2)}, u32[]{:S(2)}) collective-permute-start(f32[1024,128]{1,0:T(8,128)S(1)} %all_gather.19), channel_id=1, source_target_pairs={{0,1},{1,0},{2,3},{3,2},{4,5},{5,4},{6,7},{7,6},{8,9},{9,8},{10,11... | collective-permute-start | bytes 1572872 | tf_op jit(solution)/shard_map/ppermute | solution.py:110
  140.1 1.6 %collective-permute-done.3 = f32[1024,128]{1,0:T(8,128)S(1)} collective-permute-done((f32[1024,128]{1,0:T(8,128)S(1)}, f32[1024,128]{1,0:T(8,128)S(1)}, u32[]{:S(2)}, u32[]{:S(2)}) %collective-permute-start.3) | collective-permute-done | bytes 524320 | tf_op jit(solution)/shard_map/ppermute | solution.py:110
  141.7 1.1 maximum_select_fusion
  (21 shorter events, 0.2 us)
Async XLA Ops:
  0.7 18.0 %copy-start = (f32[2176,128]{1,0:T(8,128)S(1)}, f32[2176,128]{1,0:T(8,128)}, u32[]{:S(2)}) copy-start(f32[2176,128]{1,0:T(8,128)} %param.4) | copy-start | bytes 3342340
  1.9 62.5 %slice-start = ((f32[2304,128]{1,0:T(8,128)}), f32[128,128]{1,0:T(8,128)S(1)}, s32[]{:S(2)}) async-start(f32[2304,128]{1,0:T(8,128)} %param.3), calls=%async_computation.4 | async-start | bytes 131072 | tf_op jit(solution)/shard_map/slice | solution.py:51
  1.9 62.5 %copy-start.3 = (f32[2,64,128]{2,1,0:T(8,128)S(1)}, f32[2,64,128]{2,1,0:T(8,128)}, u32[]{:S(2)}) copy-start(f32[2,64,128]{2,1,0:T(8,128)} %param.5) | copy-start | bytes 196612
  65.4 14.1 %all-to-all-start.2 = ((f32[16,64,128]{2,1,0:T(8,128)}), f32[16,64,128]{2,1,0:T(8,128)S(1)}, u32[]{:S(2)}, u32[]{:S(2)}) async-start(f32[16,64,128]{2,1,0:T(8,128)} %broadcast_in_dim.11), calls=%async_computation.2 | async-start | bytes 1048576 | tf_op jit(solution)/shard_map/all_to_all | solution.py:16
  69.0 7.9 %copy-start.2 = (f32[2304,128]{1,0:T(8,128)S(1)}, f32[2304,128]{1,0:T(8,128)}, u32[]{:S(2)}) copy-start(f32[2304,128]{1,0:T(8,128)} %param.3) | copy-start | bytes 3538948
  69.1 18.5 %collective-permute-start.2 = (f32[512,128]{1,0:T(8,128)S(1)}, f32[512,128]{1,0:T(8,128)S(1)}, u32[]{:S(2)}, u32[]{:S(2)}) collective-permute-start(f32[512,128]{1,0:T(8,128)S(1)} %bitcast.23), channel_id=1, source_target_pairs={{0,2},{2,0},{1,3},{3,1},{4,6},{6,4},{5,7},{7,5},{8,10},{10,8},{9,1... | collective-permute-start | bytes 786440 | tf_op jit(solution)/shard_map/ppermute | solution.py:96
  71.6 16.1 %collective-permute-start = (f32[512,128]{1,0:T(8,128)S(1)}, f32[512,128]{1,0:T(8,128)S(1)}, u32[]{:S(2)}, u32[]{:S(2)}) collective-permute-start(f32[512,128]{1,0:T(8,128)S(1)} %bitcast.22), channel_id=1, source_target_pairs={{0,1},{1,0},{2,3},{3,2},{4,5},{5,4},{6,7},{7,6},{8,9},{9,8},{10,11... | collective-permute-start | bytes 786440 | tf_op jit(solution)/shard_map/ppermute | solution.py:94
  73.9 13.7 %collective-permute-start.1 = (f32[512,128]{1,0:T(8,128)S(1)}, f32[512,128]{1,0:T(8,128)S(1)}, u32[]{:S(2)}, u32[]{:S(2)}) collective-permute-start(f32[512,128]{1,0:T(8,128)S(1)} %bitcast.21), channel_id=1, source_target_pairs={{0,3},{3,0},{1,2},{2,1},{4,7},{7,4},{5,6},{6,5},{8,11},{11,8},{9,1... | collective-permute-start | bytes 786440 | tf_op jit(solution)/shard_map/ppermute | solution.py:95
  79.5 8.7 %copy-start.1 = (f32[128,128]{1,0:T(8,128)}, f32[128,128]{1,0:T(8,128)S(1)}, u32[]{:S(2)}) copy-start(f32[128,128]{1,0:T(8,128)S(1)} %pad_maximum_fusion) | copy-start | bytes 196612
  137.9 3.8 %collective-permute-start.3 = (f32[1024,128]{1,0:T(8,128)S(1)}, f32[1024,128]{1,0:T(8,128)S(1)}, u32[]{:S(2)}, u32[]{:S(2)}) collective-permute-start(f32[1024,128]{1,0:T(8,128)S(1)} %all_gather.19), channel_id=1, source_target_pairs={{0,1},{1,0},{2,3},{3,2},{4,5},{5,4},{6,7},{7,6},{8,9},{9,8},{10,11... | collective-permute-start | bytes 1572872 | tf_op jit(solution)/shard_map/ppermute | solution.py:110
